TPU v7x, 32 devices: a whole 2x2x4 slice. The times are simulated.
32 devices in a mesh: rows: 8 (over z, y), dims: 4 (over x, core).
Axes of the slice: x: 2, y: 2, z: 4, core: 2. Of those that a mesh axis runs over, the one named last changes fastest.
Arguments:
- table: bfloat16 [1, 256, 32768], P(None, 'dims', 'rows'), may hold values from -6 to 6
- accum: float32 [1, 32768], P(None, 'rows'), may hold values from 0.5 to 8
- grad_pooled: bfloat16 [1, 256, 1024], P(None, 'dims', 'rows'), may hold values from -6 to 6
- sample_slot: int32 [1, 8, 8, 1280], P(None, 'rows'), may hold values from 0 to 127
- row_slot: int32 [1, 8, 8, 1280], P(None, 'rows'), may hold values from 0 to 4095
- weight: int32 [1, 8, 8, 1280], P(None, 'rows'), may hold values from 1 to 3
- send_count: int32 [1, 8, 8], P(None, 'rows'), may hold values from 1 to 1280, as said below
Outputs:
- pooled: float32 [1, 256, 1024], P(None, 'dims', 'rows')
- new_table: bfloat16 [1, 256, 32768], P(None, 'dims', 'rows')
- new_accum: float32 [1, 32768], P(None, 'rows')
Inputs may be any that keep to these rules, and one draw needn't show every extreme that they name: `send_count`: at most 1280 live entries from one row shard to one owner per feature; in every feature one owner receives exactly 1280 from every row shard. Slots at or after the count are unused.
All inputs are finite; a program needn't handle non-finite values.
Results may differ from a plain program's by a relative error of at most 0.001.
Values may be sent and summed in bfloat16 or wider, within the bound.
No kernel may reach another device: no remote copies, remote signals or barrier semaphores. Data moves between devices by JAX's collectives and lax.ppermute only.
A program may use at most 64 MiB of HBM per device.

v0:
```python
import math

import jax
import jax.numpy as jnp
from jax import lax
from jax.sharding import PartitionSpec as P

D = 256


step_size = 0.3


def shards(table, accum, grad_pooled, sample_slot, row_slot, weight, send_count):
    feat_count, dim_local, row_local = table.shape
    peer_count = lax.axis_size("rows")
    own_samples = grad_pooled.shape[2]
    slot_count = sample_slot.shape[3]
    entry_count = peer_count * slot_count
    block_rows = math.gcd(row_local, 512)
    block_count = row_local // block_rows
    sample_local = sample_slot.reshape(feat_count, peer_count, slot_count)
    row_index = row_slot.reshape(feat_count, peer_count, slot_count)
    flat_rows = row_index.reshape(feat_count, 1, entry_count)
    live_count = send_count.reshape(feat_count, peer_count)
    slot_iota = lax.broadcasted_iota(jnp.int32, (1, 1, slot_count), 2)
    live_mask = slot_iota < live_count[:, :, None]
    weights = jnp.where(live_mask, weight.reshape(feat_count, peer_count, slot_count), 0)
    flat_weights = weights.reshape(feat_count, 1, entry_count).astype(jnp.bfloat16)
    block_iota = lax.broadcasted_iota(jnp.int32, (1, block_rows, 1), 1)

    def lookup_block(carry, block):
        start = block * block_rows
        table_part = lax.dynamic_slice_in_dim(table, start, block_rows, 2)
        selector = (flat_rows == block_iota + start).astype(jnp.bfloat16)
        return (
            carry
            + jnp.einsum("fdr,fre->fde", table_part, selector, preferred_element_type=jnp.float32),
            None,
        )

    looked_up, _ = lax.scan(
        lookup_block,
        jnp.zeros((feat_count, dim_local, entry_count), jnp.float32),
        jnp.arange(block_count, dtype=jnp.int32),
    )
    picked = looked_up.astype(jnp.bfloat16).reshape(feat_count, dim_local, peer_count, slot_count)
    positions = lax.broadcasted_iota(jnp.int32, (1, 1, 1, own_samples), 3)
    onehot = jnp.where(sample_local[..., None] == positions, weights[..., None], 0).astype(
        jnp.bfloat16
    )
    pooled = lax.psum_scatter(
        jnp.einsum("fdnk,fnkj->nfdj", picked, onehot, preferred_element_type=jnp.float32),
        "rows",
        scatter_dimension=0,
        tiled=True,
    ).reshape(feat_count, dim_local, own_samples)
    all_grads = lax.all_gather(grad_pooled, "rows", axis=2, tiled=True)
    all_grads = all_grads.reshape(feat_count, dim_local, peer_count, own_samples)
    selector = (sample_local[..., None] == positions).astype(jnp.bfloat16)
    entry_values = jnp.einsum(
        "fdnj,fnkj->fdnk", all_grads, selector, preferred_element_type=jnp.float32
    ).astype(jnp.bfloat16)
    entry_flat = entry_values.reshape(feat_count, dim_local, entry_count)

    def gradient_block(block):
        start = block * block_rows
        weighted = jnp.where(flat_rows == block_iota + start, flat_weights, 0)
        return jnp.einsum("fde,fre->fdr", entry_flat, weighted, preferred_element_type=jnp.float32)

    grad_blocks = lax.map(gradient_block, jnp.arange(block_count, dtype=jnp.int32))
    row_grad = jnp.moveaxis(grad_blocks, 0, 2).reshape(feat_count, dim_local, row_local)
    squares = jnp.sum(row_grad * row_grad, axis=1)
    norm_total = lax.psum(squares, "dims")
    new_accum = accum + norm_total / D
    new_table = (
        table.astype(jnp.float32) - step_size * row_grad / jnp.sqrt(new_accum)[:, None, :]
    ).astype(jnp.bfloat16)
    return (pooled, new_table, new_accum)


def solution(mesh):
    return jax.shard_map(
        shards,
        mesh=mesh,
        in_specs=(
            P(None, "dims", "rows"),
            P(None, "rows"),
            P(None, "dims", "rows"),
            P(None, "rows", None, None),
            P(None, "rows", None, None),
            P(None, "rows", None, None),
            P(None, "rows", None),
        ),
        out_specs=(P(None, "dims", "rows"), P(None, "dims", "rows"), P(None, "rows")),
        check_vma=False,
    )
```

profile of v0, /device:TPU:0, one launch (start us, length us, event | category | flops | bytes accessed | tf_op | source)
XLA Modules:
  0.0 151.7 jit_solution(12816893557992294160)
XLA Ops:
  7.2 0.0 reduce-scatter.2.cloned.1.call-start
  7.2 0.8 reshape_reshape.3
  8.1 48.6 %while.25 = (s32[]{:T(128)}, f32[1,64,10240]{2,1,0:T(8,128)S(1)}, s32[8]{0:T(128)S(1)}, bf16[1,64,4096]{2,1,0:T(8,128)(2,1)}, s32[1,1,10240]{2,1,0:T(1,128)S(1)}...) while((s32[]{:T(128)}, f32[1,64,10240]{2,1,0:T(8,128)S(1)}, s32[8]{0:T(128)S(1)}, ...), condition=%wide.region_1.2_spmd.clone, body=%wide.region_0.1_spmd.clone.sunk | while | flops 677642752 | bytes 5353649 | solution.py:42
  8.1 0.6 dynamic_slice.25
  9.3 4.8 %fusion.55 = f32[1,64,10240]{2,1,0:T(8,128)S(1)} fusion(s32[10240]{0:T(1024)S(1)} %bitcast.90, s32[512]{0:T(512)S(1)} %bitcast.88, f32[1,64,10240]{2,1,0:T(8,128)S(1)} %get-tuple-element.264, pred[]{:T(512)S(6)} %compare.3, bf16[1,64,4096]{2,1,0:T(8,128)(2,1)} %get-tuple-element.275, s32[]{:T(128)S(6)} %select_n.63), kind=kOutput, calls=%fused_computation.5.clone.1 | convolution fusion | flops 677642240 | bytes 5351429 | tf_op jit(solution)/shard_map/while/body/eval_jaxpr/fdr,fre->fde/dot_general | solution.py:38
  14.1 0.6 dynamic_slice.25
  15.4 4.8 %fusion.55 = f32[1,64,10240]{2,1,0:T(8,128)S(1)} fusion(s32[10240]{0:T(1024)S(1)} %bitcast.90, s32[512]{0:T(512)S(1)} %bitcast.88, f32[1,64,10240]{2,1,0:T(8,128)S(1)} %get-tuple-element.264, pred[]{:T(512)S(6)} %compare.3, bf16[1,64,4096]{2,1,0:T(8,128)(2,1)} %get-tuple-element.275, s32[]{:T(128)S(6)} %select_n.63), kind=kOutput, calls=%fused_computation.5.clone.1 | convolution fusion | flops 677642240 | bytes 5351429 | tf_op jit(solution)/shard_map/while/body/eval_jaxpr/fdr,fre->fde/dot_general | solution.py:38
  20.2 0.6 dynamic_slice.25
  21.5 4.8 %fusion.55 = f32[1,64,10240]{2,1,0:T(8,128)S(1)} fusion(s32[10240]{0:T(1024)S(1)} %bitcast.90, s32[512]{0:T(512)S(1)} %bitcast.88, f32[1,64,10240]{2,1,0:T(8,128)S(1)} %get-tuple-element.264, pred[]{:T(512)S(6)} %compare.3, bf16[1,64,4096]{2,1,0:T(8,128)(2,1)} %get-tuple-element.275, s32[]{:T(128)S(6)} %select_n.63), kind=kOutput, calls=%fused_computation.5.clone.1 | convolution fusion | flops 677642240 | bytes 5351429 | tf_op jit(solution)/shard_map/while/body/eval_jaxpr/fdr,fre->fde/dot_general | solution.py:38
  26.3 0.6 dynamic_slice.25
  27.5 4.8 %fusion.55 = f32[1,64,10240]{2,1,0:T(8,128)S(1)} fusion(s32[10240]{0:T(1024)S(1)} %bitcast.90, s32[512]{0:T(512)S(1)} %bitcast.88, f32[1,64,10240]{2,1,0:T(8,128)S(1)} %get-tuple-element.264, pred[]{:T(512)S(6)} %compare.3, bf16[1,64,4096]{2,1,0:T(8,128)(2,1)} %get-tuple-element.275, s32[]{:T(128)S(6)} %select_n.63), kind=kOutput, calls=%fused_computation.5.clone.1 | convolution fusion | flops 677642240 | bytes 5351429 | tf_op jit(solution)/shard_map/while/body/eval_jaxpr/fdr,fre->fde/dot_general | solution.py:38
  32.4 0.6 dynamic_slice.25
  33.6 4.8 %fusion.55 = f32[1,64,10240]{2,1,0:T(8,128)S(1)} fusion(s32[10240]{0:T(1024)S(1)} %bitcast.90, s32[512]{0:T(512)S(1)} %bitcast.88, f32[1,64,10240]{2,1,0:T(8,128)S(1)} %get-tuple-element.264, pred[]{:T(512)S(6)} %compare.3, bf16[1,64,4096]{2,1,0:T(8,128)(2,1)} %get-tuple-element.275, s32[]{:T(128)S(6)} %select_n.63), kind=kOutput, calls=%fused_computation.5.clone.1 | convolution fusion | flops 677642240 | bytes 5351429 | tf_op jit(solution)/shard_map/while/body/eval_jaxpr/fdr,fre->fde/dot_general | solution.py:38
  38.4 0.6 dynamic_slice.25
  39.7 4.8 %fusion.55 = f32[1,64,10240]{2,1,0:T(8,128)S(1)} fusion(s32[10240]{0:T(1024)S(1)} %bitcast.90, s32[512]{0:T(512)S(1)} %bitcast.88, f32[1,64,10240]{2,1,0:T(8,128)S(1)} %get-tuple-element.264, pred[]{:T(512)S(6)} %compare.3, bf16[1,64,4096]{2,1,0:T(8,128)(2,1)} %get-tuple-element.275, s32[]{:T(128)S(6)} %select_n.63), kind=kOutput, calls=%fused_computation.5.clone.1 | convolution fusion | flops 677642240 | bytes 5351429 | tf_op jit(solution)/shard_map/while/body/eval_jaxpr/fdr,fre->fde/dot_general | solution.py:38
  44.5 0.6 dynamic_slice.25
  45.8 4.8 %fusion.55 = f32[1,64,10240]{2,1,0:T(8,128)S(1)} fusion(s32[10240]{0:T(1024)S(1)} %bitcast.90, s32[512]{0:T(512)S(1)} %bitcast.88, f32[1,64,10240]{2,1,0:T(8,128)S(1)} %get-tuple-element.264, pred[]{:T(512)S(6)} %compare.3, bf16[1,64,4096]{2,1,0:T(8,128)(2,1)} %get-tuple-element.275, s32[]{:T(128)S(6)} %select_n.63), kind=kOutput, calls=%fused_computation.5.clone.1 | convolution fusion | flops 677642240 | bytes 5351429 | tf_op jit(solution)/shard_map/while/body/eval_jaxpr/fdr,fre->fde/dot_general | solution.py:38
  50.6 0.6 dynamic_slice.25
  51.8 4.8 %fusion.55 = f32[1,64,10240]{2,1,0:T(8,128)S(1)} fusion(s32[10240]{0:T(1024)S(1)} %bitcast.90, s32[512]{0:T(512)S(1)} %bitcast.88, f32[1,64,10240]{2,1,0:T(8,128)S(1)} %get-tuple-element.264, pred[]{:T(512)S(6)} %compare.3, bf16[1,64,4096]{2,1,0:T(8,128)(2,1)} %get-tuple-element.275, s32[]{:T(128)S(6)} %select_n.63), kind=kOutput, calls=%fused_computation.5.clone.1 | convolution fusion | flops 677642240 | bytes 5351429 | tf_op jit(solution)/shard_map/while/body/eval_jaxpr/fdr,fre->fde/dot_general | solution.py:38
  56.6 0.0 copy-start.1
  56.6 0.0 copy-start.4
  56.7 0.1 convert_element_type.41
  56.8 0.2 copy.18
  57.0 0.4 copy-done.1
  57.4 0.1 bitcast_select_fusion
  57.5 5.2 %fusion.39 = f32[8,1,64,128]{3,2,0,1:T(8,128)} fusion(s32[8,1280]{1,0:T(8,128)S(1)} %bitcast_select_fusion, s32[8,1280]{1,0:T(8,128)S(1)} %bitcast.94, bf16[64,8,1280]{2,1,0:T(8,128)(2,1)S(1)} %bitcast.82), kind=kOutput, calls=%fused_computation.34 | convolution fusion | flops 171704320 | bytes 1654784 | tf_op jit(solution)/shard_map/fdnk,fnkj->nfdj/dot_general | solution.py:53
  62.6 0.0 reduce-scatter.2.cloned.1.call-update
  62.8 0.1 lt.56
  62.9 28.1 %all_gather.3 = bf16[1,64,1024]{2,1,0:T(8,128)(2,1)S(1)} all-gather(bf16[1,64,128]{2,1,0:T(8,128)(2,1)S(1)} %copy-done.2), channel_id=1, replica_groups=mesh['rows'=8,'dims'=4] {'rows'}, dimensions={2}, use_global_device_ids=true | all-gather | bytes 147456 | tf_op jit(solution)/shard_map/all_gather | solution.py:58
  91.0 3.1 %fusion.32 = bf16[1,8,8,8,1280]{4,3,2,1,0:T(8,128)(2,1)S(1)} fusion(s32[8,1280]{1,0:T(8,128)S(1)} %bitcast.95, bf16[64,8,128]{2,1,0:T(8,128)(2,1)S(1)} %bitcast.84), kind=kOutput, calls=%fused_computation.27 | convolution fusion | flops 169738240 | bytes 1482752 | tf_op jit(solution)/shard_map/fdnj,fnkj->fdnk/dot_general | solution.py:61
  94.2 0.1 copy.16
  94.3 0.1 fusion.43
  94.3 38.5 %while.24 = (s32[]{:T(128)}, f32[8,1,64,512]{3,2,1,0:T(8,128)S(1)}, s32[1,1,10240]{2,1,0:T(1,128)S(1)}, s32[8]{0:T(128)S(1)}, bf16[1,1,10240]{2,1,0:T(2,128)(2,1...) while((s32[]{:T(128)}, f32[8,1,64,512]{3,2,1,0:T(8,128)S(1)}, ...), condition=%wide.region_4.5_spmd.clone, body=%wide.region_3.4_spmd.clone.sunk | while | flops 681574912 | bytes 1548423 | solution.py:71
  94.4 0.6 dynamic_slice.23
  95.6 0.1 reduce.5
  95.7 3.4 %fusion.52 = f32[8,1,64,512]{3,2,1,0:T(8,128)S(1)} fusion(f32[8,1,64,512]{3,2,1,0:T(8,128)S(1)} %get-tuple-element.291, s32[]{:T(128)S(6)} %copy.36, bf16[1,64,10240]{2,1,0:T(8,128)(2,1)S(1)} %get-tuple-element.304, s32[10240]{0:T(1024)S(1)} %bitcast.91, s32[512]{0:T(512)S(1)} %bitcast.89, bf16[10240]{0:T(1024)(128)(2,1)S(1)} %reduce.5), kind=kOutput, calls=%fused_computation.20.clone.1 | convolution fusion | flops 681574400 | bytes 1505284 | tf_op jit(solution)/shard_map/while/body/eval_jaxpr/fde,fre->fdr/dot_general | solution.py:69
  99.2 0.6 dynamic_slice.23
  100.4 0.1 reduce.5
  100.5 3.4 %fusion.52 = f32[8,1,64,512]{3,2,1,0:T(8,128)S(1)} fusion(f32[8,1,64,512]{3,2,1,0:T(8,128)S(1)} %get-tuple-element.291, s32[]{:T(128)S(6)} %copy.36, bf16[1,64,10240]{2,1,0:T(8,128)(2,1)S(1)} %get-tuple-element.304, s32[10240]{0:T(1024)S(1)} %bitcast.91, s32[512]{0:T(512)S(1)} %bitcast.89, bf16[10240]{0:T(1024)(128)(2,1)S(1)} %reduce.5), kind=kOutput, calls=%fused_computation.20.clone.1 | convolution fusion | flops 681574400 | bytes 1505284 | tf_op jit(solution)/shard_map/while/body/eval_jaxpr/fde,fre->fdr/dot_general | solution.py:69
  104.0 0.6 dynamic_slice.23
  105.2 0.1 reduce.5
  105.3 3.4 %fusion.52 = f32[8,1,64,512]{3,2,1,0:T(8,128)S(1)} fusion(f32[8,1,64,512]{3,2,1,0:T(8,128)S(1)} %get-tuple-element.291, s32[]{:T(128)S(6)} %copy.36, bf16[1,64,10240]{2,1,0:T(8,128)(2,1)S(1)} %get-tuple-element.304, s32[10240]{0:T(1024)S(1)} %bitcast.91, s32[512]{0:T(512)S(1)} %bitcast.89, bf16[10240]{0:T(1024)(128)(2,1)S(1)} %reduce.5), kind=kOutput, calls=%fused_computation.20.clone.1 | convolution fusion | flops 681574400 | bytes 1505284 | tf_op jit(solution)/shard_map/while/body/eval_jaxpr/fde,fre->fdr/dot_general | solution.py:69
  108.8 0.6 dynamic_slice.23
  110.0 0.1 reduce.5
  110.1 3.4 %fusion.52 = f32[8,1,64,512]{3,2,1,0:T(8,128)S(1)} fusion(f32[8,1,64,512]{3,2,1,0:T(8,128)S(1)} %get-tuple-element.291, s32[]{:T(128)S(6)} %copy.36, bf16[1,64,10240]{2,1,0:T(8,128)(2,1)S(1)} %get-tuple-element.304, s32[10240]{0:T(1024)S(1)} %bitcast.91, s32[512]{0:T(512)S(1)} %bitcast.89, bf16[10240]{0:T(1024)(128)(2,1)S(1)} %reduce.5), kind=kOutput, calls=%fused_computation.20.clone.1 | convolution fusion | flops 681574400 | bytes 1505284 | tf_op jit(solution)/shard_map/while/body/eval_jaxpr/fde,fre->fdr/dot_general | solution.py:69
  113.6 0.6 dynamic_slice.23
  114.8 0.1 reduce.5
  115.0 3.4 %fusion.52 = f32[8,1,64,512]{3,2,1,0:T(8,128)S(1)} fusion(f32[8,1,64,512]{3,2,1,0:T(8,128)S(1)} %get-tuple-element.291, s32[]{:T(128)S(6)} %copy.36, bf16[1,64,10240]{2,1,0:T(8,128)(2,1)S(1)} %get-tuple-element.304, s32[10240]{0:T(1024)S(1)} %bitcast.91, s32[512]{0:T(512)S(1)} %bitcast.89, bf16[10240]{0:T(1024)(128)(2,1)S(1)} %reduce.5), kind=kOutput, calls=%fused_computation.20.clone.1 | convolution fusion | flops 681574400 | bytes 1505284 | tf_op jit(solution)/shard_map/while/body/eval_jaxpr/fde,fre->fdr/dot_general | solution.py:69
  118.4 0.6 dynamic_slice.23
  119.7 0.1 reduce.5
  119.8 3.4 %fusion.52 = f32[8,1,64,512]{3,2,1,0:T(8,128)S(1)} fusion(f32[8,1,64,512]{3,2,1,0:T(8,128)S(1)} %get-tuple-element.291, s32[]{:T(128)S(6)} %copy.36, bf16[1,64,10240]{2,1,0:T(8,128)(2,1)S(1)} %get-tuple-element.304, s32[10240]{0:T(1024)S(1)} %bitcast.91, s32[512]{0:T(512)S(1)} %bitcast.89, bf16[10240]{0:T(1024)(128)(2,1)S(1)} %reduce.5), kind=kOutput, calls=%fused_computation.20.clone.1 | convolution fusion | flops 681574400 | bytes 1505284 | tf_op jit(solution)/shard_map/while/body/eval_jaxpr/fde,fre->fdr/dot_general | solution.py:69
  123.2 0.6 dynamic_slice.23
  124.5 0.1 reduce.5
  124.6 3.4 %fusion.52 = f32[8,1,64,512]{3,2,1,0:T(8,128)S(1)} fusion(f32[8,1,64,512]{3,2,1,0:T(8,128)S(1)} %get-tuple-element.291, s32[]{:T(128)S(6)} %copy.36, bf16[1,64,10240]{2,1,0:T(8,128)(2,1)S(1)} %get-tuple-element.304, s32[10240]{0:T(1024)S(1)} %bitcast.91, s32[512]{0:T(512)S(1)} %bitcast.89, bf16[10240]{0:T(1024)(128)(2,1)S(1)} %reduce.5), kind=kOutput, calls=%fused_computation.20.clone.1 | convolution fusion | flops 681574400 | bytes 1505284 | tf_op jit(solution)/shard_map/while/body/eval_jaxpr/fde,fre->fdr/dot_general | solution.py:69
  128.0 0.6 dynamic_slice.23
  129.3 0.1 reduce.5
  129.4 3.4 %fusion.52 = f32[8,1,64,512]{3,2,1,0:T(8,128)S(1)} fusion(f32[8,1,64,512]{3,2,1,0:T(8,128)S(1)} %get-tuple-element.291, s32[]{:T(128)S(6)} %copy.36, bf16[1,64,10240]{2,1,0:T(8,128)(2,1)S(1)} %get-tuple-element.304, s32[10240]{0:T(1024)S(1)} %bitcast.91, s32[512]{0:T(512)S(1)} %bitcast.89, bf16[10240]{0:T(1024)(128)(2,1)S(1)} %reduce.5), kind=kOutput, calls=%fused_computation.20.clone.1 | convolution fusion | flops 681574400 | bytes 1505284 | tf_op jit(solution)/shard_map/while/body/eval_jaxpr/fde,fre->fdr/dot_general | solution.py:69
  132.8 0.0 copy-start.3
  132.8 0.0 copy-start
  132.8 0.2 multiply_reduce_fusion
  133.0 0.1 copy.17
  133.1 10.1 %psum.7 = f32[1,4096]{1,0:T(1,128)S(1)} all-reduce(f32[1,4096]{1,0:T(1,128)S(1)} %bitcast.87), channel_id=1, replica_groups=mesh['rows'=8,'dims'=4] {'dims'}, use_global_device_ids=true, to_apply=%region_6.7 | all-reduce | flops 4096 | bytes 32768 | tf_op jit(solution)/shard_map/psum | solution.py:74
  143.2 0.6 fusion.45
  143.9 0.9 subtract_convert_fusion
  (34 shorter events, 0.3 us)
Async XLA Ops:
  7.2 137.7 %reduce-scatter.2.cloned.1.call-start = ((), (), s32[]{:S(2)}) async-start(), calls=%async_computation.1 | async-start | bytes 294912 | tf_op jit(solution)/shard_map/reduce_scatter | solution.py:52
  56.6 0.8 copy-start.1
  56.6 0.8 copy-start.4
  56.7 0.8 copy-start.5
  57.5 5.4 %copy-start.2 = (bf16[1,64,128]{2,1,0:T(8,128)(2,1)S(1)}, bf16[1,64,128]{2,1,0:T(8,128)(2,1)}, u32[]{:S(2)}) copy-start(bf16[1,64,128]{2,1,0:T(8,128)(2,1)} %param.13) | copy-start | bytes 49156
  132.8 10.4 %copy-start.3 = (f32[1,4096]{1,0:T(1,128)S(1)}, f32[1,4096]{1,0:T(1,128)}, u32[]{:S(2)}) copy-start(f32[1,4096]{1,0:T(1,128)} %param.12) | copy-start | bytes 49156
  132.8 11.1 %copy-start = (bf16[1,64,4096]{2,1,0:T(8,128)(2,1)S(1)}, bf16[1,64,4096]{2,1,0:T(8,128)(2,1)}, u32[]{:S(2)}) copy-start(bf16[1,64,4096]{2,1,0:T(8,128)(2,1)} %get-tuple-element.309) | copy-start | bytes 1572868
Sparse Core Ops, SparseCore 0:
  62.8 64.8 reduce-scatter.1
where the time goes:
time: 152 us
  matrix products  73.9 us (49%)
  blocking collectives  38.2 us (25%)
  between operations  14.2 us (9%)
  local copies, waits for them, and re-layouts  11.3 us (7%)
  loops' own time  11 us (7%)
  other arithmetic  3.03 us (2%)
    dot_general x8, matrix products, lookup_block(): jnp.einsum('fdr,fre->fde', table_part, selector, preferred_element_type=j...  38.3 us
    all_gather x1, blocking collectives, shards(): all_grads = lax.all_gather(grad_pooled, 'rows', axis=2, tiled=True)  28.1 us
    dot_general x8, matrix products, gradient_block(): jnp.einsum('fde,fre->fdr', entry_flat, weighted, preferred_element_type=j...  27.4 us
    psum x1, blocking collectives, shards(): norm_total = lax.psum(squares, 'dims')  10.1 us
    dynamic_slice x16, local copies, waits for them, and re-layouts, shards(): lax.scan(lookup_block, jnp.zeros((feat_count, dim_local, entry_count), jn...  9.38 us
    another operation x1, loops' own time, shards(): lax.scan(lookup_block, jnp.zeros((feat_count, dim_local, entry_count), jn...  5.55 us
    another operation x1, loops' own time, shards(): lax.map(gradient_block, jnp.arange(block_count, dtype=jnp.int32))  5.46 us
    dot_general x1, matrix products, shards(): jnp.einsum('fdnk,fnkj->nfdj', picked, onehot, preferred_element_type=jnp....  5.15 us
  transfers between devices with their start and end apart: 1, of which 0 were waited for; matrix products, arithmetic and copies ran while one was open for 25% of the time, Pallas kernels for 0%

commit v1 on v0

--- a/solution.py
+++ b/solution.py
@@ -1,17 +1,374 @@
+import functools
 import math
 
 import jax
 import jax.numpy as jnp
 from jax import lax
+from jax.experimental import pallas as pl
+from jax.experimental.pallas import tpu as pltpu
 from jax.sharding import PartitionSpec as P
 
+
 D = 256
 
 
 step_size = 0.3
 
 
+LANES = 128
+CHUNK = 256
+NARROW = jnp.float8_e4m3fn
+EXACT = 256.0
+FAST_BYTES = 24 << 20
+VMEM_LIMIT = 16 << 20
+
+
+def factor_product(row, sample, weight, count, low, span, depth):
+    row = row[:, :depth]
+    slot = lax.broadcasted_iota(jnp.int32, row.shape, 1)
+    live = jnp.where(slot < count, weight[:, :depth], 0).astype(jnp.bfloat16)
+    left_key = (row % low).astype(jnp.int16)
+    right_key = ((row // low) * LANES + sample[:, :depth]).astype(jnp.int16)
+    left_iota = lax.broadcasted_iota(jnp.int16, (low, depth), 0)
+    right_iota = lax.broadcasted_iota(jnp.int16, (span * LANES, depth), 0)
+    zero = jnp.bfloat16(0)
+    left = jnp.where(left_iota == left_key, live, zero).astype(NARROW)
+    right = jnp.where(right_iota == right_key, jnp.bfloat16(1), zero).astype(NARROW)
+    return lax.dot_general(
+        left, right, (((1,), (1,)), ((), ())), preferred_element_type=jnp.float32
+    )
+
+
+def count_kernel(
+    count_hbm, row_hbm, sample_hbm, weight_hbm, table_hbm,
+    counts_ref, pooled_ref, low_ref, flag_ref,
+    count_ref, row_ref, sample_ref, weight_ref, table_ref, peak_ref, spill_ref, sems,
+    *, masks, low, span, chunks,
+):
+    loads = [
+        pltpu.make_async_copy(source, target, sems.at[index])
+        for index, (source, target) in enumerate(
+            (
+                (count_hbm, count_ref),
+                (row_hbm, row_ref),
+                (sample_hbm, sample_ref),
+                (weight_hbm, weight_ref),
+                (table_hbm, table_ref),
+            )
+        )
+    ]
+    for load in loads:
+        load.start()
+    me = lax.axis_index("rows")
+    peak_ref[...] = jnp.zeros_like(peak_ref)
+    for load in loads[:-1]:
+        load.wait()
+
+    def owner_of(index):
+        owner = me ^ masks[0]
+        for place, mask in enumerate(masks[1:], 1):
+            owner = jnp.where(index == place, me ^ mask, owner)
+        return owner
+
+    def count_pair(pair, carry):
+        for member in range(2):
+            owner = owner_of(2 * pair + member)
+            count = count_ref[0, owner]
+            row = row_ref[pl.ds(owner, 1), :]
+            sample = sample_ref[pl.ds(owner, 1), :]
+            weight = weight_ref[pl.ds(owner, 1), :]
+            needed = jnp.maximum((count + CHUNK - 1) // CHUNK, 1)
+            for chunk in range(1, chunks + 1):
+
+                @pl.when(needed == chunk)
+                def _(chunk=chunk):
+                    depth = min(chunk * CHUNK, row.shape[1])
+                    counts = factor_product(row, sample, weight, count, low, span, depth)
+                    counts = counts.astype(jnp.bfloat16)
+                    peak = peak_ref[...]
+                    for part in range(span):
+                        piece = counts[:, part * LANES : (part + 1) * LANES]
+                        counts_ref[
+                            pair, part * low : (part + 1) * low,
+                            member * LANES : (member + 1) * LANES,
+                        ] = piece
+                        peak = jnp.maximum(peak, piece)
+                    peak_ref[...] = peak
+
+        @pl.when(pair == 0)
+        def _():
+            loads[-1].wait()
+
+        pooled = jnp.dot(table_ref[...], counts_ref[pair], preferred_element_type=jnp.float32)
+        pooled_ref[2 * pair] = pooled[:, :LANES]
+        pooled_ref[2 * pair + 1] = pooled[:, LANES:]
+        return carry
+
+    lax.fori_loop(0, len(masks) // 2, count_pair, 0)
+
+    large = jnp.max(peak_ref[...].astype(jnp.float32)) >= EXACT
+    flag_ref[0] = large.astype(jnp.int32)
+
+    @pl.when(large)
+    def _():
+        def redo(index, carry):
+            owner = owner_of(index)
+            counts = factor_product(
+                row_ref[pl.ds(owner, 1), :], sample_ref[pl.ds(owner, 1), :],
+                weight_ref[pl.ds(owner, 1), :], count_ref[0, owner], low, span, row_ref.shape[1],
+            )
+            rest = (counts - counts.astype(jnp.bfloat16).astype(jnp.float32)).astype(jnp.bfloat16)
+            for part in range(span):
+                spill_ref[part * low : (part + 1) * low, :] = rest[
+                    :, part * LANES : (part + 1) * LANES
+                ]
+            pooled_ref[index] += jnp.dot(
+                table_ref[...], spill_ref[...], preferred_element_type=jnp.float32
+            )
+            copy = pltpu.make_async_copy(spill_ref, low_ref.at[index], sems.at[0])
+            copy.start()
+            copy.wait()
+            return carry
+
+        lax.fori_loop(0, len(masks), redo, 0)
+
+
+def count_call(masks, send_count, row, sample, weight, table):
+    total = len(masks)
+    dim_local, row_local = table.shape
+    peers, slots = row.shape
+    low = math.gcd(row_local, 512)
+    span = row_local // low
+    hbm = pl.BlockSpec(memory_space=pltpu.HBM)
+    vmem = pl.BlockSpec(memory_space=pltpu.VMEM)
+    return pl.pallas_call(
+        functools.partial(
+            count_kernel, masks=masks, low=low, span=span, chunks=-(-slots // CHUNK)
+        ),
+        in_specs=[hbm] * 5,
+        out_specs=[vmem, vmem, hbm, pl.BlockSpec(memory_space=pltpu.SMEM)],
+        scratch_shapes=[
+            pltpu.SMEM((1, peers), jnp.int32),
+            pltpu.VMEM(row.shape, jnp.int32),
+            pltpu.VMEM(row.shape, jnp.int32),
+            pltpu.VMEM(row.shape, jnp.int32),
+            pltpu.VMEM(table.shape, jnp.bfloat16),
+            pltpu.VMEM((low, LANES), jnp.bfloat16),
+            pltpu.VMEM((row_local, LANES), jnp.bfloat16),
+            pltpu.SemaphoreType.DMA((5,)),
+        ],
+        out_shape=[
+            jax.ShapeDtypeStruct((total // 2, row_local, 2 * LANES), jnp.bfloat16),
+            jax.ShapeDtypeStruct((total, dim_local, LANES), jnp.float32),
+            jax.ShapeDtypeStruct((total, row_local, LANES), jnp.bfloat16),
+            jax.ShapeDtypeStruct((1,), jnp.int32),
+        ],
+        compiler_params=pltpu.CompilerParams(vmem_limit_bytes=VMEM_LIMIT),
+        name="counts",
+    )(*(pltpu.with_memory_space_constraint(x, pltpu.HBM) for x in (send_count[None], row, sample, weight, table)))
+
+
+def grad_kernel(*refs, terms, parts, pieces, block, chained, last):
+    flag_refs = refs[:parts]
+    counts_refs = refs[parts : 2 * parts]
+    low_refs = refs[2 * parts : 3 * parts]
+    grads = refs[3 * parts : 3 * parts + pieces]
+    rest = list(refs[3 * parts + pieces :])
+    before_ref = rest.pop(0) if chained else None
+    grad_ref = rest.pop(0)
+    square_ref = rest.pop(0) if last else None
+    spill_ref, sem = rest
+    row_local = grad_ref.shape[1]
+    lefts = [
+        jnp.concatenate([grads[piece][place] for piece, place in term[2:]], axis=1)
+        for term in terms
+    ]
+    for start in range(0, row_local, block):
+        rows = slice(start, start + block)
+        total = before_ref[:, rows] if chained else None
+        for left, (part, pair, *_) in zip(lefts, terms):
+            found = lax.dot_general(
+                left, counts_refs[part][pair, rows, :], (((1,), (1,)), ((), ())),
+                preferred_element_type=jnp.float32,
+            )
+            total = found if total is None else total + found
+        grad_ref[:, rows] = total
+        if last:
+            square_ref[:, rows] = jnp.sum(total * total, axis=0, keepdims=True)
+
+    for part in range(parts):
+        mine = [term for term in terms if term[0] == part]
+        if not mine:
+            continue
+
+        @pl.when(flag_refs[part][0] > 0)
+        def _(part=part, mine=mine):
+            for _, pair, *homes in mine:
+                for member, (piece, place) in enumerate(homes):
+                    copy = pltpu.make_async_copy(low_refs[part].at[2 * pair + member], spill_ref, sem)
+                    copy.start()
+                    copy.wait()
+                    for start in range(0, row_local, block):
+                        rows = slice(start, start + block)
+                        grad_ref[:, rows] += lax.dot_general(
+                            grads[piece][place], spill_ref[rows, :], (((1,), (1,)), ((), ())),
+                            preferred_element_type=jnp.float32,
+                        )
+            if last:
+                for start in range(0, row_local, block):
+                    rows = slice(start, start + block)
+                    final = grad_ref[:, rows]
+                    square_ref[:, rows] = jnp.sum(final * final, axis=0, keepdims=True)
+
+
+def grad_call(terms, flags, counts, lows, grads, before, last):
+    parts = len(counts)
+    row_local = counts[0].shape[1]
+    dim_local = grads[0].shape[1]
+    chained = before is not None
+    smem = pl.BlockSpec(memory_space=pltpu.SMEM)
+    vmem = pl.BlockSpec(memory_space=pltpu.VMEM)
+    hbm = pl.BlockSpec(memory_space=pltpu.HBM)
+    out = [jax.ShapeDtypeStruct((dim_local, row_local), jnp.float32)]
+    if last:
+        out.append(jax.ShapeDtypeStruct((1, row_local), jnp.float32))
+    return pl.pallas_call(
+        functools.partial(
+            grad_kernel, terms=terms, parts=parts, pieces=len(grads),
+            block=math.gcd(row_local, 512), chained=chained, last=last,
+        ),
+        in_specs=[smem] * parts + [vmem] * parts + [hbm] * parts + [vmem] * (len(grads) + chained),
+        out_specs=[vmem] * len(out),
+        out_shape=out,
+        scratch_shapes=[pltpu.VMEM((row_local, LANES), jnp.bfloat16), pltpu.SemaphoreType.DMA],
+        compiler_params=pltpu.CompilerParams(vmem_limit_bytes=VMEM_LIMIT),
+        name="grads",
+    )(*flags, *counts, *lows, *grads, *([before] if chained else []))
+
+
+def flip(value, axis, mask):
+    size = lax.axis_size(axis)
+    return lax.ppermute(value, axis, [(index, index ^ mask) for index in range(size)])
+
+
+def plan(peers):
+    bits = [1 << place for place in range(peers.bit_length() - 1)]
+    gather_bits = bits[-1:] + bits[:-1]
+    stages = len(bits)
+    blocks = [None] * stages
+    phases = [None] * stages
+    blocks[-1] = [0]
+    for stage in reversed(range(stages)):
+        if stage < stages - 1:
+            blocks[stage] = phases[stage + 1] + blocks[stage + 1]
+        phases[stage] = [bits[stage] ^ mask for mask in blocks[stage]]
+    return bits, gather_bits, blocks, phases
+
+
+def staged(table, grad_pooled, sample, row, weight, send_count):
+    bits, gather_bits, blocks, phases = plan(lax.axis_size("rows"))
+    stages = len(bits)
+    passes = [phases[0], blocks[0]]
+    inputs = (send_count, row, sample, weight, table)
+
+    pieces = [grad_pooled[None]]
+    homes = {0: (0, 0)}
+
+    def arrived(piece, bit):
+        for mask, (index, place) in list(homes.items()):
+            base = sum(p.shape[0] for p in pieces[:index]) + place
+            homes[mask ^ bit] = (len(pieces), base)
+        pieces.append(piece)
+
+    arrived(flip(pieces[0], "rows", gather_bits[0]), gather_bits[0])
+    counts0, partial0, low0, flag0 = count_call(passes[0], *inputs)
+    partial0, pieces[1] = lax.optimization_barrier((partial0, pieces[1]))
+    known = [set(homes)]
+    received = [flip(partial0, "rows", bits[0])]
+    if stages > 1:
+        arrived(flip(jnp.concatenate(pieces), "rows", gather_bits[1]), gather_bits[1])
+    known.append(set(homes))
+    counts1, partial1, low1, flag1 = count_call(passes[1], *inputs)
+    partial1, received[0], pieces[-1] = lax.optimization_barrier(
+        (partial1, received[0], pieces[-1])
+    )
+    total = partial1 + received[0]
+    for stage in range(1, stages):
+        take = len(phases[stage])
+        if stage + 1 < stages:
+            arrived(
+                flip(jnp.concatenate(pieces), "rows", gather_bits[stage + 1]),
+                gather_bits[stage + 1],
+            )
+        received.append(flip(total[:take], "rows", bits[stage]))
+        total = total[take:]
+        if stage < stages - 1:
+            total = total + received[-1]
+        else:
+            pooled = total[0] + received[-1][0]
+
+    flags, counts, lows = [flag0, flag1], [counts0, counts1], [low0, low1]
+    early, late = [], []
+    for part, masks in enumerate(passes):
+        for pair in range(len(masks) // 2):
+            two = masks[2 * pair : 2 * pair + 2]
+            term = (part, pair, homes[two[0]], homes[two[1]])
+            (early if set(two) <= known[1] else late).append(term)
+    row_grad = None
+    if early and late:
+        used = 1 + max(home[0] for term in early for home in term[2:])
+        (row_grad,) = grad_call(early, flags, counts, lows, pieces[:used], None, False)
+    else:
+        late = early + late
+    row_grad, square = grad_call(late, flags, counts, lows, pieces, row_grad, True)
+    return pooled, row_grad, square
+
+
+def share(square):
+    terms = [square]
+    mask = lax.axis_size("dims") // 2
+    while mask >= 1:
+        terms = terms + [flip(term, "dims", mask) for term in terms]
+        mask //= 2
+    while len(terms) > 1:
+        half = len(terms) // 2
+        terms = [terms[index] + terms[index + half] for index in range(half)]
+    return terms[0]
+
+
+def update(table, accum, row_grad, square):
+    new_accum = accum[None, :] + share(square) / D
+    scale = step_size / jnp.sqrt(new_accum)
+    new_table = (table.astype(jnp.float32) - row_grad * scale).astype(jnp.bfloat16)
+    return new_table, new_accum[0]
+
+
+def fits(table, grad_pooled, peers):
+    return (
+        peers & (peers - 1) == 0
+        and peers > 2
+        and lax.axis_size("dims") & (lax.axis_size("dims") - 1) == 0
+        and grad_pooled.shape[2] == LANES
+        and peers * table.shape[2] * LANES * 2 <= FAST_BYTES
+    )
+
+
 def shards(table, accum, grad_pooled, sample_slot, row_slot, weight, send_count):
+    peers = lax.axis_size("rows")
+    if not fits(table, grad_pooled, peers):
+        return plain(table, accum, grad_pooled, sample_slot, row_slot, weight, send_count)
+    outs = []
+    for feature in range(table.shape[0]):
+        pooled, row_grad, square = staged(
+            table[feature], grad_pooled[feature], sample_slot[feature, 0],
+            row_slot[feature, 0], weight[feature, 0], send_count[feature, 0],
+        )
+        new_table, new_accum = update(table[feature], accum[feature], row_grad, square)
+        outs.append((pooled, new_table, new_accum))
+    return tuple(jnp.stack(out) for out in zip(*outs))
+
+
+def plain(table, accum, grad_pooled, sample_slot, row_slot, weight, send_count):
     feat_count, dim_local, row_local = table.shape
     peer_count = lax.axis_size("rows")
     own_samples = grad_pooled.shape[2]

time: 152 us -> 36.6 us (0.24)
  matrix products: 73.9 us -> 0 us
  blocking collectives: 38.2 us -> 0 us
  Pallas kernels: 0 us -> 16.1 us
  between operations: 14.2 us -> 0.75 us
  loops' own time: 11 us -> 0 us
  starting transfers between devices: 0.04 us -> 10.8 us
  local copies, waits for them, and re-layouts: 11.3 us -> 0.74 us
  waiting for transfers between devices: 0.02 us -> 4.07 us
    dot_general x18 -> x0, matrix products: 73.9 us -> none  [the longest x8 38.3 us: lookup_block(): jnp.einsum('fdr,fre->fde', table_part, selector, preferred_element_type=j...]
    all_gather x1 -> x0, blocking collectives: 28.1 us -> none  [shards(): all_grads = lax.all_gather(grad_pooled, 'rows', axis=2, tiled=True)]
    pallas_call x0 -> x4, Pallas kernels: none -> 16.1 us  [the longest x2 10.7 us: count_call(): pl.pallas_call(functools.partial(count_kernel, masks=masks, low=low, span...]
    another operation x2 -> x0, loops' own time: 11 us -> none  [the longest x1 5.55 us: shards(): lax.scan(lookup_block, jnp.zeros((feat_count, dim_local, entry_count), jn...]
    ppermute x0 -> x9, starting transfers between devices: none -> 10.8 us  [flip(): lax.ppermute(value, axis, [(index, index ^ mask) for index in range(size)])]
    psum x1 -> x0, blocking collectives: 10.1 us -> none  [shards(): norm_total = lax.psum(squares, 'dims')]
    dynamic_slice x16 -> x0, local copies, waits for them, and re-layouts: 9.38 us -> none  [shards(): lax.scan(lookup_block, jnp.zeros((feat_count, dim_local, entry_count), jn...]
    ppermute x0 -> x9, waiting for transfers between devices: none -> 4.07 us  [flip(): lax.ppermute(value, axis, [(index, index ^ mask) for index in range(size)])]
  transfers between devices with their start and end apart: 1 -> 9, of which waited for: 0 -> 3; matrix products, arithmetic and copies ran while one was open for 25% -> 6% of each run, Pallas kernels for 0% -> 45%
where the time goes in v1:
time: 36.6 us; the launch traced here: 36.1 us
  Pallas kernels  16.1 us (44%)
  starting transfers between devices  10.8 us (30%)
  waiting for transfers between devices  4.07 us (11%)
  other arithmetic  3.69 us (10%)
  between operations  0.75 us (2%)
  local copies, waits for them, and re-layouts  0.74 us (2%)
    ppermute x9, starting transfers between devices, flip(): lax.ppermute(value, axis, [(index, index ^ mask) for index in range(size)])  10.8 us
    pallas_call x2, Pallas kernels, count_call(): pl.pallas_call(functools.partial(count_kernel, masks=masks, low=low, span...  10.7 us
    pallas_call x2, Pallas kernels, grad_call(): pl.pallas_call(functools.partial(grad_kernel, terms=terms, parts=parts, p...  5.45 us
    ppermute x9, waiting for transfers between devices, flip(): lax.ppermute(value, axis, [(index, index ^ mask) for index in range(size)])  4.07 us
    concatenate x2, other arithmetic, staged(): jnp.concatenate(pieces)  1.45 us
    another operation x1, other arithmetic, shards(): return tuple((jnp.stack(out) for out in zip(*outs)))  0.94 us
  transfers between devices with their start and end apart: 9, of which 3 were waited for; matrix products, arithmetic and copies ran while one was open for 6% of the time, Pallas kernels for 45%

profile of v1, /device:TPU:0, one launch (start us, length us, event | category | flops | bytes accessed | tf_op | source)
XLA Modules:
  0.0 36.1 jit_solution(9298409294876584348)
XLA Ops:
  0.6 4.1 %collective-permute-start = (bf16[1,64,128]{2,1,0:T(8,128)(2,1)}, bf16[1,64,128]{2,1,0:T(8,128)(2,1)S(1)}, u32[]{:S(2)}, u32[]{:S(2)}) collective-permute-start(bf16[1,64,128]{2,1,0:T(8,128)(2,1)} %refs_6_.3), channel_id=1, source_target_pairs={{0,16},{4,20},{8,24},{12,28},{16,0},{20,4},{24,8},{28,12},{1,17},{... | collective-permute-start | bytes 49160 | tf_op jit(solution)/shard_map/ppermute | solution.py:251
  4.8 5.5 %counts.3 = (bf16[2,4096,256]{2,1,0:T(8,128)(2,1)S(1)}, f32[4,64,128]{2,1,0:T(8,128)S(1)}, bf16[4,4096,128]{2,1,0:T(8,128)(2,1)S(1)}, s32[1]{0:T(128)}) custom-call(s32[1,8]{1,0:T(1,128)} %bitcast.18, s32[8,1280]{1,0:T(8,128)} %bitcast.11, s32[8,1280]{1,0:T(8,128)} %bitcast.13, s32[8,1280]{1,0:T(8,128)} %bitcast.15, bf16[64,4096]{1,0:T(8,128)(2,1)} %bitcast.9), custom_call_target="tpu_custom_call" | custom-call | tf_op jit(solution)/shard_map/counts/pallas_call | solution.py:144
  10.3 0.0 collective-permute-done.refs_7_
  10.3 1.6 %collective-permute-start.1 = (f32[4,64,128]{2,1,0:T(8,128)S(1)}, f32[4,64,128]{2,1,0:T(8,128)S(1)}, u32[]{:S(2)}, u32[]{:S(2)}) collective-permute-start(f32[4,64,128]{2,1,0:T(8,128)S(1)} %get-tuple-element.20), channel_id=1, source_target_pairs={{0,4},{4,0},{8,12},{12,8},{16,20},{20,16},{24,28},{28,24},{1,5},{5... | collective-permute-start | bytes 393224 | tf_op jit(solution)/shard_map/ppermute | solution.py:251
  11.9 0.7 %pad_maximum_fusion.1 = bf16[2,64,128]{2,1,0:T(8,128)(2,1)S(1)} fusion(bf16[1,64,128]{2,1,0:T(8,128)(2,1)S(1)} %collective-permute-done.refs_7_, bf16[1,64,128]{2,1,0:T(8,128)(2,1)} %refs_6_.3), kind=kLoop, calls=%fused_computation.5 | loop fusion | flops 16384 | bytes 65536 | tf_op jit(solution)/shard_map/concatenate | solution.py:289
  12.6 0.5 %collective-permute-start.2 = (bf16[2,64,128]{2,1,0:T(8,128)(2,1)S(1)}, bf16[2,64,128]{2,1,0:T(8,128)(2,1)S(1)}, u32[]{:S(2)}, u32[]{:S(2)}) collective-permute-start(bf16[2,64,128]{2,1,0:T(8,128)(2,1)S(1)} %pad_maximum_fusion.1), channel_id=1, source_target_pairs={{0,4},{4,0},{8,12},{12,8},{16,20},{20,16},{24,28},{28,24},{1,5},{5... | collective-permute-start | bytes 98312 | tf_op jit(solution)/shard_map/ppermute | solution.py:251
  13.1 5.2 %counts.2 = (bf16[2,4096,256]{2,1,0:T(8,128)(2,1)S(1)}, f32[4,64,128]{2,1,0:T(8,128)S(1)}, bf16[4,4096,128]{2,1,0:T(8,128)(2,1)S(1)}, s32[1]{0:T(128)}) custom-call(s32[1,8]{1,0:T(1,128)} %bitcast.19, s32[8,1280]{1,0:T(8,128)} %bitcast.12, s32[8,1280]{1,0:T(8,128)} %bitcast.14, s32[8,1280]{1,0:T(8,128)} %bitcast.16, bf16[64,4096]{1,0:T(8,128)(2,1)} %bitcast.10), custom_call_target="tpu_custom_call" | custom-call | tf_op jit(solution)/shard_map/counts/pallas_call | solution.py:144
  18.3 0.0 collective-permute-done.2.refs_8_
  18.3 0.0 collective-permute-done.1
  18.3 0.6 %collective-permute-start.3 = (f32[2,64,128]{2,1,0:T(8,128)S(1)}, f32[2,64,128]{2,1,0:T(8,128)S(1)}, u32[]{:S(2)}, u32[]{:S(2)}) collective-permute-start(f32[2,64,128]{2,1,0:T(8,128)S(1)} %slice.17), channel_id=1, source_target_pairs={{0,8},{4,12},{8,0},{12,4},{16,24},{20,28},{24,16},{28,20},{1,9},{5... | collective-permute-start | bytes 196616 | tf_op jit(solution)/shard_map/ppermute | solution.py:251
  18.9 0.7 %pad_maximum_fusion = bf16[4,64,128]{2,1,0:T(8,128)(2,1)S(1)} fusion(bf16[2,64,128]{2,1,0:T(8,128)(2,1)S(1)} %collective-permute-done.2.refs_8_, bf16[1,64,128]{2,1,0:T(8,128)(2,1)S(1)} %collective-permute-done.refs_7_, bf16[1,64,128]{2,1,0:T(8,128)(2,1)} %refs_6_.3), kind=kLoop, calls=%fused_computation.3 | loop fusion | flops 65536 | bytes 131072 | tf_op jit(solution)/shard_map/concatenate | solution.py:300
  19.7 1.5 %collective-permute-start.5 = (bf16[4,64,128]{2,1,0:T(8,128)(2,1)S(1)}, bf16[4,64,128]{2,1,0:T(8,128)(2,1)S(1)}, u32[]{:S(2)}, u32[]{:S(2)}) collective-permute-start(bf16[4,64,128]{2,1,0:T(8,128)(2,1)S(1)} %pad_maximum_fusion), channel_id=1, source_target_pairs={{0,8},{4,12},{8,0},{12,4},{16,24},{20,28},{24,16},{28,20},{1,9},{5... | collective-permute-start | bytes 196616 | tf_op jit(solution)/shard_map/ppermute | solution.py:251
  21.2 1.5 %collective-permute-done.3 = f32[2,64,128]{2,1,0:T(8,128)S(1)} collective-permute-done((f32[2,64,128]{2,1,0:T(8,128)S(1)}, f32[2,64,128]{2,1,0:T(8,128)S(1)}, u32[]{:S(2)}, u32[]{:S(2)}) %collective-permute-start.3) | collective-permute-done | bytes 65568 | tf_op jit(solution)/shard_map/ppermute | solution.py:251
  22.7 0.6 %collective-permute-start.4 = (f32[1,64,128]{2,1,0:T(8,128)S(1)}, f32[1,64,128]{2,1,0:T(8,128)S(1)}, u32[]{:S(2)}, u32[]{:S(2)}) collective-permute-start(f32[1,64,128]{2,1,0:T(8,128)S(1)} %slice.19), channel_id=1, source_target_pairs={{0,16},{4,20},{8,24},{12,28},{16,0},{20,4},{24,8},{28,12},{1,17},{... | collective-permute-start | bytes 98312 | tf_op jit(solution)/shard_map/ppermute | solution.py:251
  23.3 0.0 copy-start
  23.3 0.7 %copy-done = bf16[1,64,128]{2,1,0:T(8,128)(2,1)S(1)} copy-done((bf16[1,64,128]{2,1,0:T(8,128)(2,1)S(1)}, bf16[1,64,128]{2,1,0:T(8,128)(2,1)}, u32[]{:S(2)}) %copy-start) | copy-done | bytes 16408
  24.0 2.7 %grads.2.refs_10_ = f32[64,4096]{1,0:T(8,128)S(1)} custom-call(s32[1]{0:T(128)} %get-tuple-element.24.refs_0_, s32[1]{0:T(128)} %get-tuple-element.25.refs_1_, bf16[2,4096,256]{2,1,0:T(8,128)(2,1)S(1)} %get-tuple-element.26.refs_2_, bf16[2,4096,256]{2,1,0:T(8,128)(2,1)S(1)} %get-tuple-element.27.refs_3_, ...), custom_call_target="tpu_custom_call" | custom-call | tf_op jit(solution)/shard_map/grads/pallas_call | solution.py:235
  26.7 0.0 copy-start.2
  26.7 0.0 copy-start.1
  26.8 0.0 collective-permute-done.5.refs_9_
  26.8 2.8 %grads.3 = (f32[64,4096]{1,0:T(8,128)S(1)}, f32[1,4096]{1,0:T(1,128)S(1)}) custom-call(s32[1]{0:T(128)} %get-tuple-element.24.refs_0_, s32[1]{0:T(128)} %get-tuple-element.25.refs_1_, bf16[2,4096,256]{2,1,0:T(8,128)(2,1)S(1)} %get-tuple-element.26.refs_2_, bf16[2,4096,256]{2,1,0:T(8,128)(2,1)S(1)} %get-tuple-element.27.refs_3_, ...), custom_call_target="tpu_custom_call" | custom-call | tf_op jit(solution)/shard_map/grads/pallas_call | solution.py:235
  29.5 1.8 %collective-permute-start.7 = (f32[1,4096]{1,0:T(1,128)S(1)}, f32[1,4096]{1,0:T(1,128)S(1)}, u32[]{:S(2)}, u32[]{:S(2)}) collective-permute-start(f32[1,4096]{1,0:T(1,128)S(1)} %get-tuple-element.32), channel_id=1, source_target_pairs={{0,2},{1,3},{2,0},{3,1},{4,6},{5,7},{6,4},{7,5},{8,10},{9,11},{10,... | collective-permute-start | bytes 49160 | tf_op jit(solution)/shard_map/ppermute | solution.py:251
  31.4 0.0 collective-permute-start.6
  31.4 2.0 %collective-permute-done.7 = f32[1,4096]{1,0:T(1,128)S(1)} collective-permute-done((f32[1,4096]{1,0:T(1,128)S(1)}, f32[1,4096]{1,0:T(1,128)S(1)}, u32[]{:S(2)}, u32[]{:S(2)}) %collective-permute-start.7) | collective-permute-done | bytes 16416 | tf_op jit(solution)/shard_map/ppermute | solution.py:251
  33.4 0.0 collective-permute-start.8
  33.4 0.0 collective-permute-done.4
  33.4 0.6 %slice_add_fusion.1 = f32[1,64,128]{2,1,0:T(8,128)} fusion(f32[1,64,128]{2,1,0:T(8,128)S(1)} %collective-permute-done.4, f32[2,64,128]{2,1,0:T(8,128)S(1)} %slice_add_fusion), kind=kLoop, calls=%fused_computation.4 | loop fusion | flops 8192 | bytes 98304 | tf_op jit(solution)/shard_map/add | solution.py:308
  34.0 0.0 collective-permute-done.6
  34.0 0.6 %collective-permute-done.8 = f32[1,4096]{1,0:T(1,128)S(1)} collective-permute-done((f32[1,4096]{1,0:T(1,128)S(1)}, f32[1,4096]{1,0:T(1,128)S(1)}, u32[]{:S(2)}, u32[]{:S(2)}) %collective-permute-start.8) | collective-permute-done | bytes 16416 | tf_op jit(solution)/shard_map/ppermute | solution.py:251
  34.5 0.0 copy-done.2
  34.5 0.7 %rsqrt_multiply_fusion = (f32[1,4096]{1,0:T(1,128)S(1)}, f32[1,4096]{1,0:T(1,128)}) fusion(f32[1,4096]{1,0:T(1,128)S(1)} %copy-done.2, f32[1,4096]{1,0:T(1,128)S(1)} %collective-permute-done.7, f32[1,4096]{1,0:T(1,128)S(1)} %collective-permute-done.8, f32[1,4096]{1,0:T(1,128)S(1)} %get-tuple-element.32, f32[1,4096]{1,0:T(1,128)S(1)} %collective-permute-done.6), kind=kLoop, calls=%fused_computation.6 | loop fusion | flops 24576 | bytes 114688 | tf_op jit(solution)/shard_map/div | solution.py:341
  35.2 0.0 copy-done.1
  35.2 0.9 %fusion = bf16[1,64,4096]{2,1,0:T(8,128)(2,1)} fusion(f32[64,4096]{1,0:T(8,128)S(1)} %get-tuple-element.31, f32[4096]{0:T(1024)S(1)} %bitcast.17, bf16[1,64,4096]{2,1,0:T(8,128)(2,1)S(1)} %copy-done.1), kind=kLoop, calls=%fused_computation.1 | loop fusion | flops 1048576 | bytes 2113536 | tf_op jit(solution)/shard_map/stack | solution.py:368
  (4 shorter events, 0.0 us)
Async XLA Ops:
  0.6 9.6 %collective-permute-start = (bf16[1,64,128]{2,1,0:T(8,128)(2,1)}, bf16[1,64,128]{2,1,0:T(8,128)(2,1)S(1)}, u32[]{:S(2)}, u32[]{:S(2)}) collective-permute-start(bf16[1,64,128]{2,1,0:T(8,128)(2,1)} %refs_6_.3), channel_id=1, source_target_pairs={{0,16},{4,20},{8,24},{12,28},{16,0},{20,4},{24,8},{28,12},{1,17},{... | collective-permute-start | bytes 49160 | tf_op jit(solution)/shard_map/ppermute | solution.py:251
  10.3 8.0 %collective-permute-start.1 = (f32[4,64,128]{2,1,0:T(8,128)S(1)}, f32[4,64,128]{2,1,0:T(8,128)S(1)}, u32[]{:S(2)}, u32[]{:S(2)}) collective-permute-start(f32[4,64,128]{2,1,0:T(8,128)S(1)} %get-tuple-element.20), channel_id=1, source_target_pairs={{0,4},{4,0},{8,12},{12,8},{16,20},{20,16},{24,28},{28,24},{1,5},{5... | collective-permute-start | bytes 393224 | tf_op jit(solution)/shard_map/ppermute | solution.py:251
  12.6 5.7 %collective-permute-start.2 = (bf16[2,64,128]{2,1,0:T(8,128)(2,1)S(1)}, bf16[2,64,128]{2,1,0:T(8,128)(2,1)S(1)}, u32[]{:S(2)}, u32[]{:S(2)}) collective-permute-start(bf16[2,64,128]{2,1,0:T(8,128)(2,1)S(1)} %pad_maximum_fusion.1), channel_id=1, source_target_pairs={{0,4},{4,0},{8,12},{12,8},{16,20},{20,16},{24,28},{28,24},{1,5},{5... | collective-permute-start | bytes 98312 | tf_op jit(solution)/shard_map/ppermute | solution.py:251
  18.3 4.3 %collective-permute-start.3 = (f32[2,64,128]{2,1,0:T(8,128)S(1)}, f32[2,64,128]{2,1,0:T(8,128)S(1)}, u32[]{:S(2)}, u32[]{:S(2)}) collective-permute-start(f32[2,64,128]{2,1,0:T(8,128)S(1)} %slice.17), channel_id=1, source_target_pairs={{0,8},{4,12},{8,0},{12,4},{16,24},{20,28},{24,16},{28,20},{1,9},{5... | collective-permute-start | bytes 196616 | tf_op jit(solution)/shard_map/ppermute | solution.py:251
  19.7 7.1 %collective-permute-start.5 = (bf16[4,64,128]{2,1,0:T(8,128)(2,1)S(1)}, bf16[4,64,128]{2,1,0:T(8,128)(2,1)S(1)}, u32[]{:S(2)}, u32[]{:S(2)}) collective-permute-start(bf16[4,64,128]{2,1,0:T(8,128)(2,1)S(1)} %pad_maximum_fusion), channel_id=1, source_target_pairs={{0,8},{4,12},{8,0},{12,4},{16,24},{20,28},{24,16},{28,20},{1,9},{5... | collective-permute-start | bytes 196616 | tf_op jit(solution)/shard_map/ppermute | solution.py:251
  22.7 10.7 %collective-permute-start.4 = (f32[1,64,128]{2,1,0:T(8,128)S(1)}, f32[1,64,128]{2,1,0:T(8,128)S(1)}, u32[]{:S(2)}, u32[]{:S(2)}) collective-permute-start(f32[1,64,128]{2,1,0:T(8,128)S(1)} %slice.19), channel_id=1, source_target_pairs={{0,16},{4,20},{8,24},{12,28},{16,0},{20,4},{24,8},{28,12},{1,17},{... | collective-permute-start | bytes 98312 | tf_op jit(solution)/shard_map/ppermute | solution.py:251
  23.3 0.7 %copy-start = (bf16[1,64,128]{2,1,0:T(8,128)(2,1)S(1)}, bf16[1,64,128]{2,1,0:T(8,128)(2,1)}, u32[]{:S(2)}) copy-start(bf16[1,64,128]{2,1,0:T(8,128)(2,1)} %refs_6_.3) | copy-start | bytes 49156
  26.7 7.8 %copy-start.2 = (f32[1,4096]{1,0:T(1,128)S(1)}, f32[1,4096]{1,0:T(1,128)}, u32[]{:S(2)}) copy-start(f32[1,4096]{1,0:T(1,128)} %param.8) | copy-start | bytes 49156
  26.7 8.5 %copy-start.1 = (bf16[1,64,4096]{2,1,0:T(8,128)(2,1)S(1)}, bf16[1,64,4096]{2,1,0:T(8,128)(2,1)}, u32[]{:S(2)}) copy-start(bf16[1,64,4096]{2,1,0:T(8,128)(2,1)} %param.7) | copy-start | bytes 1572868
  29.5 3.8 %collective-permute-start.7 = (f32[1,4096]{1,0:T(1,128)S(1)}, f32[1,4096]{1,0:T(1,128)S(1)}, u32[]{:S(2)}, u32[]{:S(2)}) collective-permute-start(f32[1,4096]{1,0:T(1,128)S(1)} %get-tuple-element.32), channel_id=1, source_target_pairs={{0,2},{1,3},{2,0},{3,1},{4,6},{5,7},{6,4},{7,5},{8,10},{9,11},{10,... | collective-permute-start | bytes 49160 | tf_op jit(solution)/shard_map/ppermute | solution.py:251
  31.4 2.6 %collective-permute-start.6 = (f32[1,4096]{1,0:T(1,128)S(1)}, f32[1,4096]{1,0:T(1,128)S(1)}, u32[]{:S(2)}, u32[]{:S(2)}) collective-permute-start(f32[1,4096]{1,0:T(1,128)S(1)} %get-tuple-element.32), channel_id=1, source_target_pairs={{0,1},{1,0},{2,3},{3,2},{4,5},{5,4},{6,7},{7,6},{8,9},{9,8},{10,11... | collective-permute-start | bytes 49160 | tf_op jit(solution)/shard_map/ppermute | solution.py:251
  33.4 1.2 %collective-permute-start.8 = (f32[1,4096]{1,0:T(1,128)S(1)}, f32[1,4096]{1,0:T(1,128)S(1)}, u32[]{:S(2)}, u32[]{:S(2)}) collective-permute-start(f32[1,4096]{1,0:T(1,128)S(1)} %collective-permute-done.7), channel_id=1, source_target_pairs={{0,1},{1,0},{2,3},{3,2},{4,5},{5,4},{6,7},{7,6},{8,9},{9,8},{10,11... | collective-permute-start | bytes 49160 | tf_op jit(solution)/shard_map/ppermute | solution.py:251

commit v2 on v1

--- a/solution.py
+++ b/solution.py
@@ -39,30 +39,36 @@
     )
 
 
-def count_kernel(
-    count_hbm, row_hbm, sample_hbm, weight_hbm, table_hbm,
-    counts_ref, pooled_ref, low_ref, flag_ref,
-    count_ref, row_ref, sample_ref, weight_ref, table_ref, peak_ref, spill_ref, sems,
-    *, masks, low, span, chunks,
-):
-    loads = [
-        pltpu.make_async_copy(source, target, sems.at[index])
-        for index, (source, target) in enumerate(
-            (
-                (count_hbm, count_ref),
-                (row_hbm, row_ref),
-                (sample_hbm, sample_ref),
-                (weight_hbm, weight_ref),
-                (table_hbm, table_ref),
-            )
-        )
-    ]
-    for load in loads:
-        load.start()
+def count_kernel(*refs, first, masks, low, span, chunks):
+    sources = refs[:5]
+    extra = 6 if first else 0
+    if first:
+        grad_hbm = refs[5]
+        refs = refs[6:]
+    else:
+        refs = refs[5:]
+    counts_ref, pooled_ref, low_ref, peak_ref = refs[:4]
+    held = refs[4 : 4 + extra]
+    count_ref, most_ref, spill_ref, sems = refs[4 + extra :]
+    loads = []
+    if first:
+        loads = [
+            pltpu.make_async_copy(source, target, sems.at[index])
+            for index, (source, target) in enumerate(zip((*sources, grad_hbm), held))
+        ]
+        for load in loads:
+            load.start()
+        _, row_ref, sample_ref, weight_ref, table_ref = held[:5]
+        scalars = pltpu.make_async_copy(sources[0], count_ref, sems.at[6])
+    else:
+        _, row_ref, sample_ref, weight_ref, table_ref = sources
+        scalars = pltpu.make_async_copy(sources[0], count_ref, sems.at[6])
+    scalars.start()
     me = lax.axis_index("rows")
-    peak_ref[...] = jnp.zeros_like(peak_ref)
-    for load in loads[:-1]:
+    most_ref[...] = jnp.zeros_like(most_ref)
+    for load in loads[:4]:
         load.wait()
+    scalars.wait()
 
     def owner_of(index):
         owner = me ^ masks[0]
@@ -85,7 +91,7 @@
                     depth = min(chunk * CHUNK, row.shape[1])
                     counts = factor_product(row, sample, weight, count, low, span, depth)
                     counts = counts.astype(jnp.bfloat16)
-                    peak = peak_ref[...]
+                    peak = most_ref[...]
                     for part in range(span):
                         piece = counts[:, part * LANES : (part + 1) * LANES]
                         counts_ref[
@@ -93,11 +99,14 @@
                             member * LANES : (member + 1) * LANES,
                         ] = piece
                         peak = jnp.maximum(peak, piece)
-                    peak_ref[...] = peak
-
-        @pl.when(pair == 0)
-        def _():
-            loads[-1].wait()
+                    most_ref[...] = peak
+
+        if first:
+
+            @pl.when(pair == 0)
+            def _():
+                for load in loads[4:]:
+                    load.wait()
 
         pooled = jnp.dot(table_ref[...], counts_ref[pair], preferred_element_type=jnp.float32)
         pooled_ref[2 * pair] = pooled[:, :LANES]
@@ -106,10 +115,12 @@
 
     lax.fori_loop(0, len(masks) // 2, count_pair, 0)
 
-    large = jnp.max(peak_ref[...].astype(jnp.float32)) >= EXACT
-    flag_ref[0] = large.astype(jnp.int32)
-
-    @pl.when(large)
+    most = most_ref[0:16, :]
+    for start in range(16, low, 16):
+        most = jnp.maximum(most, most_ref[start : start + 16, :])
+    peak_ref[...] = most.astype(jnp.float32)
+
+    @pl.when(jnp.max(peak_ref[...]) >= EXACT)
     def _():
         def redo(index, carry):
             owner = owner_of(index)
@@ -133,39 +144,45 @@
         lax.fori_loop(0, len(masks), redo, 0)
 
 
-def count_call(masks, send_count, row, sample, weight, table):
+def count_call(masks, operands, grad, peers):
+    first = grad is not None
+    _, row, _, _, table = operands
     total = len(masks)
     dim_local, row_local = table.shape
-    peers, slots = row.shape
+    slots = row.shape[1]
     low = math.gcd(row_local, 512)
     span = row_local // low
     hbm = pl.BlockSpec(memory_space=pltpu.HBM)
     vmem = pl.BlockSpec(memory_space=pltpu.VMEM)
+    if first:
+        arguments = [
+            pltpu.with_memory_space_constraint(value, pltpu.HBM) for value in (*operands, grad)
+        ]
+    else:
+        arguments = list(operands)
+    held = [jax.ShapeDtypeStruct(value.shape, value.dtype) for value in arguments] if first else []
     return pl.pallas_call(
         functools.partial(
-            count_kernel, masks=masks, low=low, span=span, chunks=-(-slots // CHUNK)
+            count_kernel, first=first, masks=masks, low=low, span=span, chunks=-(-slots // CHUNK)
         ),
-        in_specs=[hbm] * 5,
-        out_specs=[vmem, vmem, hbm, pl.BlockSpec(memory_space=pltpu.SMEM)],
+        in_specs=[hbm if first else vmem] * len(arguments),
+        out_specs=[vmem, vmem, hbm, vmem] + [vmem] * len(held),
         scratch_shapes=[
             pltpu.SMEM((1, peers), jnp.int32),
-            pltpu.VMEM(row.shape, jnp.int32),
-            pltpu.VMEM(row.shape, jnp.int32),
-            pltpu.VMEM(row.shape, jnp.int32),
-            pltpu.VMEM(table.shape, jnp.bfloat16),
             pltpu.VMEM((low, LANES), jnp.bfloat16),
             pltpu.VMEM((row_local, LANES), jnp.bfloat16),
-            pltpu.SemaphoreType.DMA((5,)),
+            pltpu.SemaphoreType.DMA((7,)),
         ],
         out_shape=[
             jax.ShapeDtypeStruct((total // 2, row_local, 2 * LANES), jnp.bfloat16),
             jax.ShapeDtypeStruct((total, dim_local, LANES), jnp.float32),
             jax.ShapeDtypeStruct((total, row_local, LANES), jnp.bfloat16),
-            jax.ShapeDtypeStruct((1,), jnp.int32),
-        ],
+            jax.ShapeDtypeStruct((16, LANES), jnp.float32),
+        ]
+        + held,
         compiler_params=pltpu.CompilerParams(vmem_limit_bytes=VMEM_LIMIT),
         name="counts",
-    )(*(pltpu.with_memory_space_constraint(x, pltpu.HBM) for x in (send_count[None], row, sample, weight, table)))
+    )(*arguments)
 
 
 def grad_kernel(*refs, terms, parts, pieces, block, chained, last):
@@ -201,7 +218,7 @@
         if not mine:
             continue
 
-        @pl.when(flag_refs[part][0] > 0)
+        @pl.when(jnp.max(flag_refs[part][...]) >= EXACT)
         def _(part=part, mine=mine):
             for _, pair, *homes in mine:
                 for member, (piece, place) in enumerate(homes):
@@ -226,7 +243,6 @@
     row_local = counts[0].shape[1]
     dim_local = grads[0].shape[1]
     chained = before is not None
-    smem = pl.BlockSpec(memory_space=pltpu.SMEM)
     vmem = pl.BlockSpec(memory_space=pltpu.VMEM)
     hbm = pl.BlockSpec(memory_space=pltpu.HBM)
     out = [jax.ShapeDtypeStruct((dim_local, row_local), jnp.float32)]
@@ -237,7 +253,7 @@
             grad_kernel, terms=terms, parts=parts, pieces=len(grads),
             block=math.gcd(row_local, 512), chained=chained, last=last,
         ),
-        in_specs=[smem] * parts + [vmem] * parts + [hbm] * parts + [vmem] * (len(grads) + chained),
+        in_specs=[vmem] * parts + [vmem] * parts + [hbm] * parts + [vmem] * (len(grads) + chained),
         out_specs=[vmem] * len(out),
         out_shape=out,
         scratch_shapes=[pltpu.VMEM((row_local, LANES), jnp.bfloat16), pltpu.SemaphoreType.DMA],
@@ -269,7 +285,7 @@
     bits, gather_bits, blocks, phases = plan(lax.axis_size("rows"))
     stages = len(bits)
     passes = [phases[0], blocks[0]]
-    inputs = (send_count, row, sample, weight, table)
+    peers = lax.axis_size("rows")
 
     pieces = [grad_pooled[None]]
     homes = {0: (0, 0)}
@@ -281,14 +297,17 @@
         pieces.append(piece)
 
     arrived(flip(pieces[0], "rows", gather_bits[0]), gather_bits[0])
-    counts0, partial0, low0, flag0 = count_call(passes[0], *inputs)
+    counts0, partial0, low0, flag0, *held = count_call(
+        passes[0], (send_count[None], row, sample, weight, table), pieces[0], peers
+    )
+    pieces[0] = held.pop()
     partial0, pieces[1] = lax.optimization_barrier((partial0, pieces[1]))
     known = [set(homes)]
     received = [flip(partial0, "rows", bits[0])]
     if stages > 1:
         arrived(flip(jnp.concatenate(pieces), "rows", gather_bits[1]), gather_bits[1])
     known.append(set(homes))
-    counts1, partial1, low1, flag1 = count_call(passes[1], *inputs)
+    counts1, partial1, low1, flag1 = count_call(passes[1], tuple(held), None, peers)
     partial1, received[0], pieces[-1] = lax.optimization_barrier(
         (partial1, received[0], pieces[-1])
     )
@@ -304,8 +323,6 @@
         total = total[take:]
         if stage < stages - 1:
             total = total + received[-1]
-        else:
-            pooled = total[0] + received[-1][0]
 
     flags, counts, lows = [flag0, flag1], [counts0, counts1], [low0, low1]
     early, late = [], []
@@ -321,7 +338,7 @@
     else:
         late = early + late
     row_grad, square = grad_call(late, flags, counts, lows, pieces, row_grad, True)
-    return pooled, row_grad, square
+    return (total, received[-1]), row_grad, square
 
 
 def share(square):
@@ -330,17 +347,67 @@
     while mask >= 1:
         terms = terms + [flip(term, "dims", mask) for term in terms]
         mask //= 2
-    while len(terms) > 1:
-        half = len(terms) // 2
-        terms = [terms[index] + terms[index + half] for index in range(half)]
-    return terms[0]
-
-
-def update(table, accum, row_grad, square):
-    new_accum = accum[None, :] + share(square) / D
-    scale = step_size / jnp.sqrt(new_accum)
-    new_table = (table.astype(jnp.float32) - row_grad * scale).astype(jnp.bfloat16)
-    return new_table, new_accum[0]
+    return terms
+
+
+def update_kernel(*refs, count, block):
+    terms = refs[:count]
+    accum_ref, table_ref, grad_ref, own_ref, other_ref = refs[count : count + 5]
+    pooled_hbm, table_hbm, accum_hbm, pooled_ref, new_ref, total_ref, sems = refs[count + 5 :]
+    copies = [pltpu.make_async_copy(pooled_ref, pooled_hbm, sems.at[0])]
+    pooled_ref[...] = own_ref[...] + other_ref[...]
+    copies[0].start()
+    row_local = grad_ref.shape[1]
+    for index, start in enumerate(range(0, row_local, block)):
+        rows = slice(start, start + block)
+        sums = [term[:, rows] for term in terms]
+        while len(sums) > 1:
+            half = len(sums) // 2
+            sums = [sums[place] + sums[place + half] for place in range(half)]
+        total = accum_ref[:, rows] + sums[0] / D
+        total_ref[:, rows] = total
+        scale = step_size / jnp.sqrt(total)
+        new_ref[:, rows] = (
+            table_ref[:, rows].astype(jnp.float32) - grad_ref[:, rows] * scale
+        ).astype(jnp.bfloat16)
+        copies.append(
+            pltpu.make_async_copy(
+                new_ref.at[:, pl.ds(start, block)], table_hbm.at[:, pl.ds(start, block)],
+                sems.at[1 + index],
+            )
+        )
+        copies[-1].start()
+    copies.append(pltpu.make_async_copy(total_ref, accum_hbm, sems.at[len(copies)]))
+    copies[-1].start()
+    for copy in copies:
+        copy.wait()
+
+
+def update(table, accum, row_grad, square, sums):
+    terms = share(square)
+    row_local = table.shape[1]
+    block = math.gcd(row_local, 1024)
+    hbm = pl.BlockSpec(memory_space=pltpu.HBM)
+    vmem = pl.BlockSpec(memory_space=pltpu.VMEM)
+    pooled, new_table, new_accum = pl.pallas_call(
+        functools.partial(update_kernel, count=len(terms), block=block),
+        in_specs=[vmem] * (len(terms) + 5),
+        out_specs=[hbm] * 3,
+        out_shape=[
+            jax.ShapeDtypeStruct(sums[0].shape, jnp.float32),
+            jax.ShapeDtypeStruct(table.shape, table.dtype),
+            jax.ShapeDtypeStruct((1, row_local), jnp.float32),
+        ],
+        scratch_shapes=[
+            pltpu.VMEM(sums[0].shape, jnp.float32),
+            pltpu.VMEM(table.shape, table.dtype),
+            pltpu.VMEM((1, row_local), jnp.float32),
+            pltpu.SemaphoreType.DMA((row_local // block + 2,)),
+        ],
+        compiler_params=pltpu.CompilerParams(vmem_limit_bytes=VMEM_LIMIT),
+        name="update",
+    )(*terms, accum[None], table, row_grad, *sums)
+    return pooled[0], new_table, new_accum[0]
 
 
 def fits(table, grad_pooled, peers):
@@ -359,12 +426,11 @@
         return plain(table, accum, grad_pooled, sample_slot, row_slot, weight, send_count)
     outs = []
     for feature in range(table.shape[0]):
-        pooled, row_grad, square = staged(
+        sums, row_grad, square = staged(
             table[feature], grad_pooled[feature], sample_slot[feature, 0],
             row_slot[feature, 0], weight[feature, 0], send_count[feature, 0],
         )
-        new_table, new_accum = update(table[feature], accum[feature], row_grad, square)
-        outs.append((pooled, new_table, new_accum))
+        outs.append(update(table[feature], accum[feature], row_grad, square, sums))
     return tuple(jnp.stack(out) for out in zip(*outs))
 
 

time: 36.6 us -> 29.1 us (0.80)
  other arithmetic: 3.69 us -> 0.04 us
  Pallas kernels: 16.1 us -> 13.3 us
  local copies, waits for them, and re-layouts: 0.74 us -> 0.03 us
  starting transfers between devices: 10.8 us -> 10.2 us
  waiting for transfers between devices: 4.07 us -> 4.48 us
    pallas_call x2, Pallas kernels: 5.45 us -> 3.05 us  [grad_call(): pl.pallas_call(functools.partial(grad_kernel, terms=terms, parts=parts, p...]
    concatenate x2, other arithmetic: 1.45 us -> 0.01 us  [staged(): jnp.concatenate(pieces)]
    another operation x1 -> x0, other arithmetic: 0.94 us -> none  [shards(): return tuple((jnp.stack(out) for out in zip(*outs)))]
    unnamed x6 -> x4, local copies, waits for them, and re-layouts: 0.73 us -> 0.01 us
    div x1 -> x0, other arithmetic: 0.66 us -> none  [update(): scale = step_size / jnp.sqrt(new_accum)]
    add x1 -> x0, other arithmetic: 0.62 us -> none  [staged(): pooled = total[0] + received[-1][0]]
    ppermute x9, starting transfers between devices: 10.8 us -> 10.2 us  [flip(): lax.ppermute(value, axis, [(index, index ^ mask) for index in range(size)])]
    ppermute x9, waiting for transfers between devices: 4.07 us -> 4.48 us  [flip(): lax.ppermute(value, axis, [(index, index ^ mask) for index in range(size)])]
  transfers between devices with their start and end apart: 9 -> 9, of which waited for: 3 -> 4; matrix products, arithmetic and copies ran while one was open for 6% -> 0% of each run, Pallas kernels for 45% -> 43%
where the time goes in v2:
time: 29.1 us; the launch traced here: 29 us
  Pallas kernels  13.3 us (46%)
  starting transfers between devices  10.2 us (35%)
  waiting for transfers between devices  4.48 us (15%)
  between operations  0.9 us (3%)
    ppermute x9, starting transfers between devices, flip(): lax.ppermute(value, axis, [(index, index ^ mask) for index in range(size)])  10.2 us
    pallas_call x2, Pallas kernels, count_call(): pl.pallas_call(functools.partial(count_kernel, first=first, masks=masks,...  9.39 us
    ppermute x9, waiting for transfers between devices, flip(): lax.ppermute(value, axis, [(index, index ^ mask) for index in range(size)])  4.48 us
    pallas_call x2, Pallas kernels, grad_call(): pl.pallas_call(functools.partial(grad_kernel, terms=terms, parts=parts, p...  3.05 us
    pallas_call x1, Pallas kernels, update(): pl.pallas_call(functools.partial(update_kernel, count=len(terms), block=b...  0.9 us
  transfers between devices with their start and end apart: 9, of which 4 were waited for; matrix products, arithmetic and copies ran while one was open for 0% of the time, Pallas kernels for 43%

profile of v2, /device:TPU:0, one launch (start us, length us, event | category | flops | bytes accessed | tf_op | source)
XLA Modules:
  0.0 29.0 jit_solution(8595599396706141715)
XLA Ops:
  0.6 4.1 %collective-permute-start = (bf16[1,64,128]{2,1,0:T(8,128)(2,1)}, bf16[1,64,128]{2,1,0:T(8,128)(2,1)S(1)}, u32[]{:S(2)}, u32[]{:S(2)}) collective-permute-start(bf16[1,64,128]{2,1,0:T(8,128)(2,1)} %refs_5_.1), channel_id=1, source_target_pairs={{0,16},{4,20},{8,24},{12,28},{16,0},{20,4},{24,8},{28,12},{1,17},{... | collective-permute-start | bytes 49160 | tf_op jit(solution)/shard_map/ppermute | solution.py:267
  4.8 5.0 %counts.2 = (bf16[2,4096,256]{2,1,0:T(8,128)(2,1)S(1)}, f32[4,64,128]{2,1,0:T(8,128)S(1)}, bf16[4,4096,128]{2,1,0:T(8,128)(2,1)S(1)}, f32[16,128]{1,0:T(8,128)S(...) custom-call(s32[1,8]{1,0:T(1,128)} %bitcast.11, ...), custom_call_target="tpu_custom_call" | custom-call | tf_op jit(solution)/shard_map/counts/pallas_call | solution.py:164
  9.8 0.0 collective-permute-done.refs_7_
  9.8 1.6 %collective-permute-start.1 = (f32[4,64,128]{2,1,0:T(8,128)S(1)}, f32[4,64,128]{2,1,0:T(8,128)S(1)}, u32[]{:S(2)}, u32[]{:S(2)}) collective-permute-start(f32[4,64,128]{2,1,0:T(8,128)S(1)} %get-tuple-element.42), channel_id=1, source_target_pairs={{0,4},{4,0},{8,12},{12,8},{16,20},{20,16},{24,28},{28,24},{1,5},{5... | collective-permute-start | bytes 393224 | tf_op jit(solution)/shard_map/ppermute | solution.py:267
  11.4 0.5 %collective-permute-start.2 = (bf16[2,64,128]{2,1,0:T(8,128)(2,1)S(1)}, bf16[2,64,128]{2,1,0:T(8,128)(2,1)S(1)}, u32[]{:S(2)}, u32[]{:S(2)}) collective-permute-start(bf16[2,64,128]{2,1,0:T(8,128)(2,1)S(1)} %pad_maximum_fusion.1), channel_id=1, source_target_pairs={{0,4},{4,0},{8,12},{12,8},{16,20},{20,16},{24,28},{28,24},{1,5},{5... | collective-permute-start | bytes 98312 | tf_op jit(solution)/shard_map/ppermute | solution.py:267
  11.9 4.4 %counts.3 = (bf16[2,4096,256]{2,1,0:T(8,128)(2,1)S(1)}, f32[4,64,128]{2,1,0:T(8,128)S(1)}, bf16[4,4096,128]{2,1,0:T(8,128)(2,1)S(1)}, f32[16,128]{1,0:T(8,128)S(1)}) custom-call(s32[1,8]{1,0:T(1,128)S(1)} %get-tuple-element.28.refs_0_, s32[8,1280]{1,0:T(8,128)S(1)} %get-tuple-element.29.refs_1_, s32[8,1280]{1,0:T(8,128)S(1)} %get-tuple-element.30.refs_2_, ...), custom_call_target="tpu_custom_call" | custom-call | tf_op jit(solution)/shard_map/counts/pallas_call | solution.py:164
  16.3 0.0 collective-permute-done.2.refs_8_
  16.3 0.0 collective-permute-done.1
  16.3 0.7 %collective-permute-start.7 = (f32[2,64,128]{2,1,0:T(8,128)S(1)}, f32[2,64,128]{2,1,0:T(8,128)S(1)}, u32[]{:S(2)}, u32[]{:S(2)}) collective-permute-start(f32[2,64,128]{2,1,0:T(8,128)S(1)} %slice.17), channel_id=1, source_target_pairs={{0,8},{4,12},{8,0},{12,4},{16,24},{20,28},{24,16},{28,20},{1,9},{5... | collective-permute-start | bytes 196616 | tf_op jit(solution)/shard_map/ppermute | solution.py:267
  17.0 1.5 %collective-permute-start.3 = (bf16[4,64,128]{2,1,0:T(8,128)(2,1)S(1)}, bf16[4,64,128]{2,1,0:T(8,128)(2,1)S(1)}, u32[]{:S(2)}, u32[]{:S(2)}) collective-permute-start(bf16[4,64,128]{2,1,0:T(8,128)(2,1)S(1)} %pad_maximum_fusion), channel_id=1, source_target_pairs={{0,8},{4,12},{8,0},{12,4},{16,24},{20,28},{24,16},{28,20},{1,9},{5... | collective-permute-start | bytes 196616 | tf_op jit(solution)/shard_map/ppermute | solution.py:267
  18.5 1.5 %grads.2.refs_10_ = f32[64,4096]{1,0:T(8,128)S(1)} custom-call(f32[16,128]{1,0:T(8,128)S(1)} %get-tuple-element.27.refs_0_, f32[16,128]{1,0:T(8,128)S(1)} %get-tuple-element.33.refs_1_, bf16[2,4096,256]{2,1,0:T(8,128)(2,1)S(1)} %get-tuple-element.34.refs_2_, bf16[2,4096,256]{2,1,0:T(8,128)(2,1)S(1)} %get-tuple-element.35.refs_3_, ...), custom_call_target="tpu_custom_call" | custom-call | tf_op jit(solution)/shard_map/grads/pallas_call | solution.py:251
  20.0 0.6 %collective-permute-done.7 = f32[2,64,128]{2,1,0:T(8,128)S(1)} collective-permute-done((f32[2,64,128]{2,1,0:T(8,128)S(1)}, f32[2,64,128]{2,1,0:T(8,128)S(1)}, u32[]{:S(2)}, u32[]{:S(2)}) %collective-permute-start.7) | collective-permute-done | bytes 65568 | tf_op jit(solution)/shard_map/ppermute | solution.py:267
  20.7 0.0 copy-start
  20.7 0.0 copy-start.1
  20.7 0.2 collective-permute-start.8
  21.0 0.4 %collective-permute-done.3.refs_9_ = bf16[4,64,128]{2,1,0:T(8,128)(2,1)S(1)} collective-permute-done((bf16[4,64,128]{2,1,0:T(8,128)(2,1)S(1)}, bf16[4,64,128]{2,1,0:T(8,128)(2,1)S(1)}, u32[]{:S(2)}, u32[]{:S(2)}) %collective-permute-start.3) | collective-permute-done | bytes 65568 | tf_op jit(solution)/shard_map/ppermute | solution.py:267
  21.4 1.5 %grads.3 = (f32[64,4096]{1,0:T(8,128)S(1)}, f32[1,4096]{1,0:T(1,128)S(1)}) custom-call(f32[16,128]{1,0:T(8,128)S(1)} %get-tuple-element.27.refs_0_, f32[16,128]{1,0:T(8,128)S(1)} %get-tuple-element.33.refs_1_, bf16[2,4096,256]{2,1,0:T(8,128)(2,1)S(1)} %get-tuple-element.34.refs_2_, bf16[2,4096,256]{2,1,0:T(8,128)(2,1)S(1)} %get-tuple-element.35.refs_3_, ...), custom_call_target="tpu_custom_call" | custom-call | tf_op jit(solution)/shard_map/grads/pallas_call | solution.py:251
  22.9 1.6 %collective-permute-start.4 = (f32[1,4096]{1,0:T(1,128)S(1)}, f32[1,4096]{1,0:T(1,128)S(1)}, u32[]{:S(2)}, u32[]{:S(2)}) collective-permute-start(f32[1,4096]{1,0:T(1,128)S(1)} %get-tuple-element.44.refs_0_), channel_id=1, source_target_pairs={{0,2},{1,3},{2,0},{3,1},{4,6},{5,7},{6,4},{7,5},{8,10},{9,11},{10,... | collective-permute-start | bytes 49160 | tf_op jit(solution)/shard_map/ppermute | solution.py:267
  24.5 0.0 collective-permute-start.5
  24.5 2.2 %collective-permute-done.4.refs_1_ = f32[1,4096]{1,0:T(1,128)S(1)} collective-permute-done((f32[1,4096]{1,0:T(1,128)S(1)}, f32[1,4096]{1,0:T(1,128)S(1)}, u32[]{:S(2)}, u32[]{:S(2)}) %collective-permute-start.4) | collective-permute-done | bytes 16416 | tf_op jit(solution)/shard_map/ppermute | solution.py:267
  26.7 0.0 collective-permute-start.6
  26.7 0.0 collective-permute-done.5.refs_2_
  26.7 0.0 collective-permute-done.8.refs_8_
  26.7 1.2 %collective-permute-done.6.refs_3_ = f32[1,4096]{1,0:T(1,128)S(1)} collective-permute-done((f32[1,4096]{1,0:T(1,128)S(1)}, f32[1,4096]{1,0:T(1,128)S(1)}, u32[]{:S(2)}, u32[]{:S(2)}) %collective-permute-start.6) | collective-permute-done | bytes 16416 | tf_op jit(solution)/shard_map/ppermute | solution.py:267
  27.9 0.0 copy-done
  27.9 0.0 copy-done.1
  27.9 0.9 %update.1 = (f32[1,64,128]{2,1,0:T(8,128)}, bf16[64,4096]{1,0:T(8,128)(2,1)}, f32[1,4096]{1,0:T(1,128)}) custom-call(f32[1,4096]{1,0:T(1,128)S(1)} %get-tuple-element.44.refs_0_, f32[1,4096]{1,0:T(1,128)S(1)} %collective-permute-done.4.refs_1_, f32[1,4096]{1,0:T(1,128)S(1)} %collective-permute-done.5.refs_2_, f32[1,4096]{1,0:T(1,128)S(1)} %collective-permute-done.6.refs_3_, ...), custom_call_target="tpu_custom_call" | custom-call | tf_op jit(solution)/shard_map/update/pallas_call | solution.py:392
  (6 shorter events, 0.1 us)
Async XLA Ops:
  0.6 9.2 %collective-permute-start = (bf16[1,64,128]{2,1,0:T(8,128)(2,1)}, bf16[1,64,128]{2,1,0:T(8,128)(2,1)S(1)}, u32[]{:S(2)}, u32[]{:S(2)}) collective-permute-start(bf16[1,64,128]{2,1,0:T(8,128)(2,1)} %refs_5_.1), channel_id=1, source_target_pairs={{0,16},{4,20},{8,24},{12,28},{16,0},{20,4},{24,8},{28,12},{1,17},{... | collective-permute-start | bytes 49160 | tf_op jit(solution)/shard_map/ppermute | solution.py:267
  9.8 6.5 %collective-permute-start.1 = (f32[4,64,128]{2,1,0:T(8,128)S(1)}, f32[4,64,128]{2,1,0:T(8,128)S(1)}, u32[]{:S(2)}, u32[]{:S(2)}) collective-permute-start(f32[4,64,128]{2,1,0:T(8,128)S(1)} %get-tuple-element.42), channel_id=1, source_target_pairs={{0,4},{4,0},{8,12},{12,8},{16,20},{20,16},{24,28},{28,24},{1,5},{5... | collective-permute-start | bytes 393224 | tf_op jit(solution)/shard_map/ppermute | solution.py:267
  11.4 4.9 %collective-permute-start.2 = (bf16[2,64,128]{2,1,0:T(8,128)(2,1)S(1)}, bf16[2,64,128]{2,1,0:T(8,128)(2,1)S(1)}, u32[]{:S(2)}, u32[]{:S(2)}) collective-permute-start(bf16[2,64,128]{2,1,0:T(8,128)(2,1)S(1)} %pad_maximum_fusion.1), channel_id=1, source_target_pairs={{0,4},{4,0},{8,12},{12,8},{16,20},{20,16},{24,28},{28,24},{1,5},{5... | collective-permute-start | bytes 98312 | tf_op jit(solution)/shard_map/ppermute | solution.py:267
  16.3 4.3 %collective-permute-start.7 = (f32[2,64,128]{2,1,0:T(8,128)S(1)}, f32[2,64,128]{2,1,0:T(8,128)S(1)}, u32[]{:S(2)}, u32[]{:S(2)}) collective-permute-start(f32[2,64,128]{2,1,0:T(8,128)S(1)} %slice.17), channel_id=1, source_target_pairs={{0,8},{4,12},{8,0},{12,4},{16,24},{20,28},{24,16},{28,20},{1,9},{5... | collective-permute-start | bytes 196616 | tf_op jit(solution)/shard_map/ppermute | solution.py:267
  17.0 4.3 %collective-permute-start.3 = (bf16[4,64,128]{2,1,0:T(8,128)(2,1)S(1)}, bf16[4,64,128]{2,1,0:T(8,128)(2,1)S(1)}, u32[]{:S(2)}, u32[]{:S(2)}) collective-permute-start(bf16[4,64,128]{2,1,0:T(8,128)(2,1)S(1)} %pad_maximum_fusion), channel_id=1, source_target_pairs={{0,8},{4,12},{8,0},{12,4},{16,24},{20,28},{24,16},{28,20},{1,9},{5... | collective-permute-start | bytes 196616 | tf_op jit(solution)/shard_map/ppermute | solution.py:267
  20.7 7.2 %copy-start = (bf16[1,64,4096]{2,1,0:T(8,128)(2,1)S(1)}, bf16[1,64,4096]{2,1,0:T(8,128)(2,1)}, u32[]{:S(2)}) copy-start(bf16[1,64,4096]{2,1,0:T(8,128)(2,1)} %param.7) | copy-start | bytes 1572868
  20.7 7.2 %copy-start.1 = (f32[1,4096]{1,0:T(1,128)S(1)}, f32[1,4096]{1,0:T(1,128)}, u32[]{:S(2)}) copy-start(f32[1,4096]{1,0:T(1,128)} %refs_4_.1) | copy-start | bytes 49156
  20.7 6.0 %collective-permute-start.8 = (f32[1,64,128]{2,1,0:T(8,128)S(1)}, f32[1,64,128]{2,1,0:T(8,128)S(1)}, u32[]{:S(2)}, u32[]{:S(2)}) collective-permute-start(f32[1,64,128]{2,1,0:T(8,128)S(1)} %get-tuple-element.51), channel_id=1, source_target_pairs={{0,16},{4,20},{8,24},{12,28},{16,0},{20,4},{24,8},{28,12},{1,17},{... | collective-permute-start | bytes 98312 | tf_op jit(solution)/shard_map/ppermute | solution.py:267
  22.9 3.8 %collective-permute-start.4 = (f32[1,4096]{1,0:T(1,128)S(1)}, f32[1,4096]{1,0:T(1,128)S(1)}, u32[]{:S(2)}, u32[]{:S(2)}) collective-permute-start(f32[1,4096]{1,0:T(1,128)S(1)} %get-tuple-element.44.refs_0_), channel_id=1, source_target_pairs={{0,2},{1,3},{2,0},{3,1},{4,6},{5,7},{6,4},{7,5},{8,10},{9,11},{10,... | collective-permute-start | bytes 49160 | tf_op jit(solution)/shard_map/ppermute | solution.py:267
  24.5 2.3 %collective-permute-start.5 = (f32[1,4096]{1,0:T(1,128)S(1)}, f32[1,4096]{1,0:T(1,128)S(1)}, u32[]{:S(2)}, u32[]{:S(2)}) collective-permute-start(f32[1,4096]{1,0:T(1,128)S(1)} %get-tuple-element.44.refs_0_), channel_id=1, source_target_pairs={{0,1},{1,0},{2,3},{3,2},{4,5},{5,4},{6,7},{7,6},{8,9},{9,8},{10,11... | collective-permute-start | bytes 49160 | tf_op jit(solution)/shard_map/ppermute | solution.py:267
  26.7 1.2 %collective-permute-start.6 = (f32[1,4096]{1,0:T(1,128)S(1)}, f32[1,4096]{1,0:T(1,128)S(1)}, u32[]{:S(2)}, u32[]{:S(2)}) collective-permute-start(f32[1,4096]{1,0:T(1,128)S(1)} %collective-permute-done.4.refs_1_), channel_id=1, source_target_pairs={{0,1},{1,0},{2,3},{3,2},{4,5},{5,4},{6,7},{7,6},{8,9},{9,8},{10,11... | collective-permute-start | bytes 49160 | tf_op jit(solution)/shard_map/ppermute | solution.py:267

commit v3 on v2

--- a/solution.py
+++ b/solution.py
@@ -47,9 +47,10 @@
         refs = refs[6:]
     else:
         refs = refs[5:]
-    counts_ref, pooled_ref, low_ref, peak_ref = refs[:4]
+    counts_ref, out_ref, low_ref, peak_ref = refs[:4]
     held = refs[4 : 4 + extra]
-    count_ref, most_ref, spill_ref, sems = refs[4 + extra :]
+    count_ref, most_ref, spill_ref, sum_ref, sems = refs[4 + extra :]
+    pooled_ref = sum_ref if first else out_ref
     loads = []
     if first:
         loads = [
@@ -142,6 +143,12 @@
             return carry
 
         lax.fori_loop(0, len(masks), redo, 0)
+
+    if first:
+        sums = sum_ref[...]
+        head = sums.astype(jnp.bfloat16)
+        out_ref[: len(masks)] = head
+        out_ref[len(masks) :] = (sums - head.astype(jnp.float32)).astype(jnp.bfloat16)
 
 
 def count_call(masks, operands, grad, peers):
@@ -171,11 +178,14 @@
             pltpu.SMEM((1, peers), jnp.int32),
             pltpu.VMEM((low, LANES), jnp.bfloat16),
             pltpu.VMEM((row_local, LANES), jnp.bfloat16),
+            pltpu.VMEM((total, dim_local, LANES), jnp.float32),
             pltpu.SemaphoreType.DMA((7,)),
         ],
         out_shape=[
             jax.ShapeDtypeStruct((total // 2, row_local, 2 * LANES), jnp.bfloat16),
-            jax.ShapeDtypeStruct((total, dim_local, LANES), jnp.float32),
+            jax.ShapeDtypeStruct((2 * total, dim_local, LANES), jnp.bfloat16)
+            if first
+            else jax.ShapeDtypeStruct((total, dim_local, LANES), jnp.float32),
             jax.ShapeDtypeStruct((total, row_local, LANES), jnp.bfloat16),
             jax.ShapeDtypeStruct((16, LANES), jnp.float32),
         ]
@@ -288,49 +298,56 @@
     peers = lax.axis_size("rows")
 
     pieces = [grad_pooled[None]]
-    homes = {0: (0, 0)}
+    homes = [(0, (0, 0))]
+
+    def gathered():
+        sizes = [sum(home[0] == index for _, home in homes) for index in range(len(pieces))]
+        return [piece[:size] for piece, size in zip(pieces, sizes)]
 
     def arrived(piece, bit):
-        for mask, (index, place) in list(homes.items()):
-            base = sum(p.shape[0] for p in pieces[:index]) + place
-            homes[mask ^ bit] = (len(pieces), base)
+        homes.extend(
+            [(mask ^ bit, (len(pieces), place)) for place, (mask, _) in enumerate(homes)]
+        )
         pieces.append(piece)
 
     arrived(flip(pieces[0], "rows", gather_bits[0]), gather_bits[0])
-    counts0, partial0, low0, flag0, *held = count_call(
+    counts0, halves, low0, flag0, *held = count_call(
         passes[0], (send_count[None], row, sample, weight, table), pieces[0], peers
     )
     pieces[0] = held.pop()
-    partial0, pieces[1] = lax.optimization_barrier((partial0, pieces[1]))
-    known = [set(homes)]
-    received = [flip(partial0, "rows", bits[0])]
-    if stages > 1:
-        arrived(flip(jnp.concatenate(pieces), "rows", gather_bits[1]), gather_bits[1])
-    known.append(set(homes))
+    halves, pieces[1] = lax.optimization_barrier((halves, pieces[1]))
+    sent = len(homes)
+    message = flip(jnp.concatenate(gathered() + [halves]), "rows", bits[0])
+    arrived(message, gather_bits[1])
+    known = {mask for mask, _ in homes}
     counts1, partial1, low1, flag1 = count_call(passes[1], tuple(held), None, peers)
-    partial1, received[0], pieces[-1] = lax.optimization_barrier(
-        (partial1, received[0], pieces[-1])
-    )
-    total = partial1 + received[0]
+    partial1, message = lax.optimization_barrier((partial1, message))
+    pieces[-1] = message
+    half = len(passes[0])
+    total = partial1 + (
+        message[sent : sent + half].astype(jnp.float32)
+        + message[sent + half :].astype(jnp.float32)
+    )
     for stage in range(1, stages):
         take = len(phases[stage])
         if stage + 1 < stages:
             arrived(
-                flip(jnp.concatenate(pieces), "rows", gather_bits[stage + 1]),
+                flip(jnp.concatenate(gathered()), "rows", gather_bits[stage + 1]),
                 gather_bits[stage + 1],
             )
-        received.append(flip(total[:take], "rows", bits[stage]))
+        incoming = flip(total[:take], "rows", bits[stage])
         total = total[take:]
         if stage < stages - 1:
-            total = total + received[-1]
+            total = total + incoming
 
     flags, counts, lows = [flag0, flag1], [counts0, counts1], [low0, low1]
+    spots = dict(homes)
     early, late = [], []
     for part, masks in enumerate(passes):
         for pair in range(len(masks) // 2):
             two = masks[2 * pair : 2 * pair + 2]
-            term = (part, pair, homes[two[0]], homes[two[1]])
-            (early if set(two) <= known[1] else late).append(term)
+            term = (part, pair, spots[two[0]], spots[two[1]])
+            (early if set(two) <= known else late).append(term)
     row_grad = None
     if early and late:
         used = 1 + max(home[0] for term in early for home in term[2:])
@@ -338,7 +355,7 @@
     else:
         late = early + late
     row_grad, square = grad_call(late, flags, counts, lows, pieces, row_grad, True)
-    return (total, received[-1]), row_grad, square
+    return (total, incoming), row_grad, square
 
 
 def share(square):

time: 29.1 us -> 29.1 us (level)
    ppermute x9 -> x8, starting transfers between devices: 10.2 us -> 9.98 us  [flip(): lax.ppermute(value, axis, [(index, index ^ mask) for index in range(size)])]
    ppermute x9 -> x8, waiting for transfers between devices: 4.48 us -> 4.59 us  [flip(): lax.ppermute(value, axis, [(index, index ^ mask) for index in range(size)])]
  transfers between devices with their start and end apart: 9 -> 8, of which waited for: 4 -> 4; matrix products, arithmetic and copies ran while one was open for 0% -> 0% of each run, Pallas kernels for 43% -> 43%
where the time goes in v3:
time: 29.1 us; the launch traced here: 28.9 us
  Pallas kernels  13.4 us (46%)
  starting transfers between devices  9.98 us (34%)
  waiting for transfers between devices  4.59 us (16%)
  between operations  0.91 us (3%)
    ppermute x8, starting transfers between devices, flip(): lax.ppermute(value, axis, [(index, index ^ mask) for index in range(size)])  9.98 us
    pallas_call x2, Pallas kernels, count_call(): pl.pallas_call(functools.partial(count_kernel, first=first, masks=masks,...  9.4 us
    ppermute x8, waiting for transfers between devices, flip(): lax.ppermute(value, axis, [(index, index ^ mask) for index in range(size)])  4.59 us
    pallas_call x2, Pallas kernels, grad_call(): pl.pallas_call(functools.partial(grad_kernel, terms=terms, parts=parts, p...  3.05 us
    pallas_call x1, Pallas kernels, update(): pl.pallas_call(functools.partial(update_kernel, count=len(terms), block=b...  0.9 us
  transfers between devices with their start and end apart: 8, of which 4 were waited for; matrix products, arithmetic and copies ran while one was open for 0% of the time, Pallas kernels for 43%

profile of v3, /device:TPU:0, one launch (start us, length us, event | category | flops | bytes accessed | tf_op | source)
XLA Modules:
  0.0 28.9 jit_solution(15645253173649191383)
XLA Ops:
  0.6 4.1 %collective-permute-start = (bf16[1,64,128]{2,1,0:T(8,128)(2,1)}, bf16[1,64,128]{2,1,0:T(8,128)(2,1)S(1)}, u32[]{:S(2)}, u32[]{:S(2)}) collective-permute-start(bf16[1,64,128]{2,1,0:T(8,128)(2,1)} %refs_5_.1), channel_id=1, source_target_pairs={{0,16},{4,20},{8,24},{12,28},{16,0},{20,4},{24,8},{28,12},{1,17},{... | collective-permute-start | bytes 49160 | tf_op jit(solution)/shard_map/ppermute | solution.py:277
  4.8 5.0 %counts.2 = (bf16[2,4096,256]{2,1,0:T(8,128)(2,1)S(1)}, bf16[8,64,128]{2,1,0:T(8,128)(2,1)S(1)}, bf16[4,4096,128]{2,1,0:T(8,128)(2,1)S(1)}, f32[16,128]{1,0:T(8,...) custom-call(s32[1,8]{1,0:T(1,128)} %bitcast.11, ...), custom_call_target="tpu_custom_call" | custom-call | tf_op jit(solution)/shard_map/counts/pallas_call | solution.py:171
  9.8 0.0 collective-permute-done.refs_7_
  9.8 1.6 %collective-permute-start.1 = (bf16[10,64,128]{2,1,0:T(8,128)(2,1)S(1)}, bf16[10,64,128]{2,1,0:T(8,128)(2,1)S(1)}, u32[]{:S(2)}, u32[]{:S(2)}) collective-permute-start(bf16[10,64,128]{2,1,0:T(8,128)(2,1)S(1)} %pad_maximum_fusion), channel_id=1, source_target_pairs={{0,4},{4,0},{8,12},{12,8},{16,20},{20,16},{24,28},{28,24},{1,5},{5... | collective-permute-start | bytes 491528 | tf_op jit(solution)/shard_map/ppermute | solution.py:277
  11.4 4.4 %counts.3 = (bf16[2,4096,256]{2,1,0:T(8,128)(2,1)S(1)}, f32[4,64,128]{2,1,0:T(8,128)S(1)}, bf16[4,4096,128]{2,1,0:T(8,128)(2,1)S(1)}, f32[16,128]{1,0:T(8,128)S(1)}) custom-call(s32[1,8]{1,0:T(1,128)S(1)} %get-tuple-element.27.refs_0_, s32[8,1280]{1,0:T(8,128)S(1)} %get-tuple-element.28.refs_1_, s32[8,1280]{1,0:T(8,128)S(1)} %get-tuple-element.29.refs_2_, ...), custom_call_target="tpu_custom_call" | custom-call | tf_op jit(solution)/shard_map/counts/pallas_call | solution.py:171
  15.8 0.0 collective-permute-done.1.refs_8_
  15.9 1.1 %collective-permute-start.6 = (f32[2,64,128]{2,1,0:T(8,128)S(1)}, f32[2,64,128]{2,1,0:T(8,128)S(1)}, u32[]{:S(2)}, u32[]{:S(2)}) collective-permute-start(f32[2,64,128]{2,1,0:T(8,128)S(1)} %slice.29), channel_id=1, source_target_pairs={{0,8},{4,12},{8,0},{12,4},{16,24},{20,28},{24,16},{28,20},{1,9},{5... | collective-permute-start | bytes 196616 | tf_op jit(solution)/shard_map/ppermute | solution.py:277
  17.0 1.1 %collective-permute-start.2 = (bf16[4,64,128]{2,1,0:T(8,128)(2,1)S(1)}, bf16[4,64,128]{2,1,0:T(8,128)(2,1)S(1)}, u32[]{:S(2)}, u32[]{:S(2)}) collective-permute-start(bf16[4,64,128]{2,1,0:T(8,128)(2,1)S(1)} %pad_maximum_fusion.1), channel_id=1, source_target_pairs={{0,8},{4,12},{8,0},{12,4},{16,24},{20,28},{24,16},{28,20},{1,9},{5... | collective-permute-start | bytes 196616 | tf_op jit(solution)/shard_map/ppermute | solution.py:277
  18.1 1.5 %grads.2.refs_10_ = f32[64,4096]{1,0:T(8,128)S(1)} custom-call(f32[16,128]{1,0:T(8,128)S(1)} %get-tuple-element.26.refs_0_, f32[16,128]{1,0:T(8,128)S(1)} %get-tuple-element.32.refs_1_, bf16[2,4096,256]{2,1,0:T(8,128)(2,1)S(1)} %get-tuple-element.33.refs_2_, bf16[2,4096,256]{2,1,0:T(8,128)(2,1)S(1)} %get-tuple-element.34.refs_3_, ...), custom_call_target="tpu_custom_call" | custom-call | tf_op jit(solution)/shard_map/grads/pallas_call | solution.py:261
  19.6 0.6 %collective-permute-done.6 = f32[2,64,128]{2,1,0:T(8,128)S(1)} collective-permute-done((f32[2,64,128]{2,1,0:T(8,128)S(1)}, f32[2,64,128]{2,1,0:T(8,128)S(1)}, u32[]{:S(2)}, u32[]{:S(2)}) %collective-permute-start.6) | collective-permute-done | bytes 65568 | tf_op jit(solution)/shard_map/ppermute | solution.py:277
  20.2 0.0 copy-start
  20.3 0.0 copy-start.1
  20.3 0.5 %collective-permute-start.7 = (f32[1,64,128]{2,1,0:T(8,128)S(1)}, f32[1,64,128]{2,1,0:T(8,128)S(1)}, u32[]{:S(2)}, u32[]{:S(2)}) collective-permute-start(f32[1,64,128]{2,1,0:T(8,128)S(1)} %get-tuple-element.49), channel_id=1, source_target_pairs={{0,16},{4,20},{8,24},{12,28},{16,0},{20,4},{24,8},{28,12},{1,17},{... | collective-permute-start | bytes 98312 | tf_op jit(solution)/shard_map/ppermute | solution.py:277
  20.8 0.5 %collective-permute-done.2.refs_9_ = bf16[4,64,128]{2,1,0:T(8,128)(2,1)S(1)} collective-permute-done((bf16[4,64,128]{2,1,0:T(8,128)(2,1)S(1)}, bf16[4,64,128]{2,1,0:T(8,128)(2,1)S(1)}, u32[]{:S(2)}, u32[]{:S(2)}) %collective-permute-start.2) | collective-permute-done | bytes 65568 | tf_op jit(solution)/shard_map/ppermute | solution.py:277
  21.3 1.5 %grads.3 = (f32[64,4096]{1,0:T(8,128)S(1)}, f32[1,4096]{1,0:T(1,128)S(1)}) custom-call(f32[16,128]{1,0:T(8,128)S(1)} %get-tuple-element.26.refs_0_, f32[16,128]{1,0:T(8,128)S(1)} %get-tuple-element.32.refs_1_, bf16[2,4096,256]{2,1,0:T(8,128)(2,1)S(1)} %get-tuple-element.33.refs_2_, bf16[2,4096,256]{2,1,0:T(8,128)(2,1)S(1)} %get-tuple-element.34.refs_3_, ...), custom_call_target="tpu_custom_call" | custom-call | tf_op jit(solution)/shard_map/grads/pallas_call | solution.py:261
  22.9 1.6 %collective-permute-start.3 = (f32[1,4096]{1,0:T(1,128)S(1)}, f32[1,4096]{1,0:T(1,128)S(1)}, u32[]{:S(2)}, u32[]{:S(2)}) collective-permute-start(f32[1,4096]{1,0:T(1,128)S(1)} %get-tuple-element.43.refs_0_), channel_id=1, source_target_pairs={{0,2},{1,3},{2,0},{3,1},{4,6},{5,7},{6,4},{7,5},{8,10},{9,11},{10,... | collective-permute-start | bytes 49160 | tf_op jit(solution)/shard_map/ppermute | solution.py:277
  24.4 0.0 collective-permute-start.4
  24.4 2.2 %collective-permute-done.3.refs_1_ = f32[1,4096]{1,0:T(1,128)S(1)} collective-permute-done((f32[1,4096]{1,0:T(1,128)S(1)}, f32[1,4096]{1,0:T(1,128)S(1)}, u32[]{:S(2)}, u32[]{:S(2)}) %collective-permute-start.3) | collective-permute-done | bytes 16416 | tf_op jit(solution)/shard_map/ppermute | solution.py:277
  26.7 0.0 collective-permute-start.5
  26.7 0.0 collective-permute-done.4.refs_2_
  26.7 0.0 collective-permute-done.7.refs_8_
  26.7 1.2 %collective-permute-done.5.refs_3_ = f32[1,4096]{1,0:T(1,128)S(1)} collective-permute-done((f32[1,4096]{1,0:T(1,128)S(1)}, f32[1,4096]{1,0:T(1,128)S(1)}, u32[]{:S(2)}, u32[]{:S(2)}) %collective-permute-start.5) | collective-permute-done | bytes 16416 | tf_op jit(solution)/shard_map/ppermute | solution.py:277
  27.9 0.0 copy-done
  27.9 0.0 copy-done.1
  27.9 0.9 %update.1 = (f32[1,64,128]{2,1,0:T(8,128)}, bf16[64,4096]{1,0:T(8,128)(2,1)}, f32[1,4096]{1,0:T(1,128)}) custom-call(f32[1,4096]{1,0:T(1,128)S(1)} %get-tuple-element.43.refs_0_, f32[1,4096]{1,0:T(1,128)S(1)} %collective-permute-done.3.refs_1_, f32[1,4096]{1,0:T(1,128)S(1)} %collective-permute-done.4.refs_2_, f32[1,4096]{1,0:T(1,128)S(1)} %collective-permute-done.5.refs_3_, ...), custom_call_target="tpu_custom_call" | custom-call | tf_op jit(solution)/shard_map/update/pallas_call | solution.py:409
  (7 shorter events, 0.1 us)
Async XLA Ops:
  0.6 9.2 %collective-permute-start = (bf16[1,64,128]{2,1,0:T(8,128)(2,1)}, bf16[1,64,128]{2,1,0:T(8,128)(2,1)S(1)}, u32[]{:S(2)}, u32[]{:S(2)}) collective-permute-start(bf16[1,64,128]{2,1,0:T(8,128)(2,1)} %refs_5_.1), channel_id=1, source_target_pairs={{0,16},{4,20},{8,24},{12,28},{16,0},{20,4},{24,8},{28,12},{1,17},{... | collective-permute-start | bytes 49160 | tf_op jit(solution)/shard_map/ppermute | solution.py:277
  9.8 6.0 %collective-permute-start.1 = (bf16[10,64,128]{2,1,0:T(8,128)(2,1)S(1)}, bf16[10,64,128]{2,1,0:T(8,128)(2,1)S(1)}, u32[]{:S(2)}, u32[]{:S(2)}) collective-permute-start(bf16[10,64,128]{2,1,0:T(8,128)(2,1)S(1)} %pad_maximum_fusion), channel_id=1, source_target_pairs={{0,4},{4,0},{8,12},{12,8},{16,20},{20,16},{24,28},{28,24},{1,5},{5... | collective-permute-start | bytes 491528 | tf_op jit(solution)/shard_map/ppermute | solution.py:277
  15.9 4.3 %collective-permute-start.6 = (f32[2,64,128]{2,1,0:T(8,128)S(1)}, f32[2,64,128]{2,1,0:T(8,128)S(1)}, u32[]{:S(2)}, u32[]{:S(2)}) collective-permute-start(f32[2,64,128]{2,1,0:T(8,128)S(1)} %slice.29), channel_id=1, source_target_pairs={{0,8},{4,12},{8,0},{12,4},{16,24},{20,28},{24,16},{28,20},{1,9},{5... | collective-permute-start | bytes 196616 | tf_op jit(solution)/shard_map/ppermute | solution.py:277
  17.0 4.3 %collective-permute-start.2 = (bf16[4,64,128]{2,1,0:T(8,128)(2,1)S(1)}, bf16[4,64,128]{2,1,0:T(8,128)(2,1)S(1)}, u32[]{:S(2)}, u32[]{:S(2)}) collective-permute-start(bf16[4,64,128]{2,1,0:T(8,128)(2,1)S(1)} %pad_maximum_fusion.1), channel_id=1, source_target_pairs={{0,8},{4,12},{8,0},{12,4},{16,24},{20,28},{24,16},{28,20},{1,9},{5... | collective-permute-start | bytes 196616 | tf_op jit(solution)/shard_map/ppermute | solution.py:277
  20.2 7.6 %copy-start = (bf16[1,64,4096]{2,1,0:T(8,128)(2,1)S(1)}, bf16[1,64,4096]{2,1,0:T(8,128)(2,1)}, u32[]{:S(2)}) copy-start(bf16[1,64,4096]{2,1,0:T(8,128)(2,1)} %param.7) | copy-start | bytes 1572868
  20.3 7.6 %copy-start.1 = (f32[1,4096]{1,0:T(1,128)S(1)}, f32[1,4096]{1,0:T(1,128)}, u32[]{:S(2)}) copy-start(f32[1,4096]{1,0:T(1,128)} %refs_4_.1) | copy-start | bytes 49156
  20.3 6.4 %collective-permute-start.7 = (f32[1,64,128]{2,1,0:T(8,128)S(1)}, f32[1,64,128]{2,1,0:T(8,128)S(1)}, u32[]{:S(2)}, u32[]{:S(2)}) collective-permute-start(f32[1,64,128]{2,1,0:T(8,128)S(1)} %get-tuple-element.49), channel_id=1, source_target_pairs={{0,16},{4,20},{8,24},{12,28},{16,0},{20,4},{24,8},{28,12},{1,17},{... | collective-permute-start | bytes 98312 | tf_op jit(solution)/shard_map/ppermute | solution.py:277
  22.9 3.8 %collective-permute-start.3 = (f32[1,4096]{1,0:T(1,128)S(1)}, f32[1,4096]{1,0:T(1,128)S(1)}, u32[]{:S(2)}, u32[]{:S(2)}) collective-permute-start(f32[1,4096]{1,0:T(1,128)S(1)} %get-tuple-element.43.refs_0_), channel_id=1, source_target_pairs={{0,2},{1,3},{2,0},{3,1},{4,6},{5,7},{6,4},{7,5},{8,10},{9,11},{10,... | collective-permute-start | bytes 49160 | tf_op jit(solution)/shard_map/ppermute | solution.py:277
  24.4 2.3 %collective-permute-start.4 = (f32[1,4096]{1,0:T(1,128)S(1)}, f32[1,4096]{1,0:T(1,128)S(1)}, u32[]{:S(2)}, u32[]{:S(2)}) collective-permute-start(f32[1,4096]{1,0:T(1,128)S(1)} %get-tuple-element.43.refs_0_), channel_id=1, source_target_pairs={{0,1},{1,0},{2,3},{3,2},{4,5},{5,4},{6,7},{7,6},{8,9},{9,8},{10,11... | collective-permute-start | bytes 49160 | tf_op jit(solution)/shard_map/ppermute | solution.py:277
  26.7 1.2 %collective-permute-start.5 = (f32[1,4096]{1,0:T(1,128)S(1)}, f32[1,4096]{1,0:T(1,128)S(1)}, u32[]{:S(2)}, u32[]{:S(2)}) collective-permute-start(f32[1,4096]{1,0:T(1,128)S(1)} %collective-permute-done.3.refs_1_), channel_id=1, source_target_pairs={{0,1},{1,0},{2,3},{3,2},{4,5},{5,4},{6,7},{7,6},{8,9},{9,8},{10,11... | collective-permute-start | bytes 49160 | tf_op jit(solution)/shard_map/ppermute | solution.py:277

commit v4 on v3

--- a/solution.py
+++ b/solution.py
@@ -39,7 +39,7 @@
     )
 
 
-def count_kernel(*refs, first, masks, low, span, chunks):
+def count_kernel(*refs, first, masks, now, low, span, chunks):
     sources = refs[:5]
     extra = 6 if first else 0
     if first:
@@ -71,11 +71,14 @@
         load.wait()
     scalars.wait()
 
+    odd = lax.axis_index("dims") % 2
+
     def owner_of(index):
-        owner = me ^ masks[0]
+        even_mask, odd_mask = masks[0], crossed(masks[0])
         for place, mask in enumerate(masks[1:], 1):
-            owner = jnp.where(index == place, me ^ mask, owner)
-        return owner
+            even_mask = jnp.where(index == place, mask, even_mask)
+            odd_mask = jnp.where(index == place, crossed(mask), odd_mask)
+        return me ^ jnp.where(odd == 1, odd_mask, even_mask)
 
     def count_pair(pair, carry):
         for member in range(2):
@@ -109,9 +112,19 @@
                 for load in loads[4:]:
                     load.wait()
 
-        pooled = jnp.dot(table_ref[...], counts_ref[pair], preferred_element_type=jnp.float32)
-        pooled_ref[2 * pair] = pooled[:, :LANES]
-        pooled_ref[2 * pair + 1] = pooled[:, LANES:]
+        @pl.when(pair < now)
+        def _():
+            pooled = jnp.dot(table_ref[...], counts_ref[pair], preferred_element_type=jnp.float32)
+            pooled_ref[2 * pair] = pooled[:, :LANES]
+            pooled_ref[2 * pair + 1] = pooled[:, LANES:]
+
+        if now < len(masks) // 2:
+
+            @pl.when(pair >= now)
+            def _():
+                pooled_ref[2 * pair] = jnp.zeros(pooled_ref.shape[1:], jnp.float32)
+                pooled_ref[2 * pair + 1] = jnp.zeros(pooled_ref.shape[1:], jnp.float32)
+
         return carry
 
     lax.fori_loop(0, len(masks) // 2, count_pair, 0)
@@ -151,7 +164,7 @@
         out_ref[len(masks) :] = (sums - head.astype(jnp.float32)).astype(jnp.bfloat16)
 
 
-def count_call(masks, operands, grad, peers):
+def count_call(masks, now, operands, grad, peers):
     first = grad is not None
     _, row, _, _, table = operands
     total = len(masks)
@@ -170,7 +183,8 @@
     held = [jax.ShapeDtypeStruct(value.shape, value.dtype) for value in arguments] if first else []
     return pl.pallas_call(
         functools.partial(
-            count_kernel, first=first, masks=masks, low=low, span=span, chunks=-(-slots // CHUNK)
+            count_kernel, first=first, masks=masks, now=now, low=low, span=span,
+            chunks=-(-slots // CHUNK),
         ),
         in_specs=[hbm if first else vmem] * len(arguments),
         out_specs=[vmem, vmem, hbm, vmem] + [vmem] * len(held),
@@ -195,15 +209,28 @@
     )(*arguments)
 
 
-def grad_kernel(*refs, terms, parts, pieces, block, chained, last):
+def grad_kernel(*refs, terms, parts, pieces, block, chained, last, pool):
     flag_refs = refs[:parts]
     counts_refs = refs[parts : 2 * parts]
     low_refs = refs[2 * parts : 3 * parts]
     grads = refs[3 * parts : 3 * parts + pieces]
     rest = list(refs[3 * parts + pieces :])
     before_ref = rest.pop(0) if chained else None
+    if pool is not None:
+        table_ref, partial_ref = rest.pop(0), rest.pop(0)
     grad_ref = rest.pop(0)
     square_ref = rest.pop(0) if last else None
+    if pool is not None:
+        pooled_ref = rest.pop(0)
+        for index, pair in enumerate(range(pool, counts_refs[1].shape[0])):
+            pooled = jnp.dot(
+                table_ref[...], counts_refs[1][pair], preferred_element_type=jnp.float32
+            )
+            for member in range(2):
+                pooled_ref[2 * index + member] = (
+                    partial_ref[2 * pair + member]
+                    + pooled[:, member * LANES : (member + 1) * LANES]
+                )
     spill_ref, sem = rest
     row_local = grad_ref.shape[1]
     lefts = [
@@ -248,7 +275,7 @@
                     square_ref[:, rows] = jnp.sum(final * final, axis=0, keepdims=True)
 
 
-def grad_call(terms, flags, counts, lows, grads, before, last):
+def grad_call(terms, flags, counts, lows, grads, before, last, pool=None, extra=()):
     parts = len(counts)
     row_local = counts[0].shape[1]
     dim_local = grads[0].shape[1]
@@ -258,23 +285,40 @@
     out = [jax.ShapeDtypeStruct((dim_local, row_local), jnp.float32)]
     if last:
         out.append(jax.ShapeDtypeStruct((1, row_local), jnp.float32))
+    if pool is not None:
+        late = 2 * (counts[1].shape[0] - pool)
+        out.append(jax.ShapeDtypeStruct((late, dim_local, LANES), jnp.float32))
     return pl.pallas_call(
         functools.partial(
-            grad_kernel, terms=terms, parts=parts, pieces=len(grads),
+            grad_kernel, terms=terms, pool=pool, parts=parts, pieces=len(grads),
             block=math.gcd(row_local, 512), chained=chained, last=last,
         ),
-        in_specs=[vmem] * parts + [vmem] * parts + [hbm] * parts + [vmem] * (len(grads) + chained),
+        in_specs=[vmem] * parts + [vmem] * parts + [hbm] * parts + [vmem] * (len(grads) + chained + len(extra)),
         out_specs=[vmem] * len(out),
         out_shape=out,
         scratch_shapes=[pltpu.VMEM((row_local, LANES), jnp.bfloat16), pltpu.SemaphoreType.DMA],
         compiler_params=pltpu.CompilerParams(vmem_limit_bytes=VMEM_LIMIT),
         name="grads",
-    )(*flags, *counts, *lows, *grads, *([before] if chained else []))
-
-
-def flip(value, axis, mask):
-    size = lax.axis_size(axis)
-    return lax.ppermute(value, axis, [(index, index ^ mask) for index in range(size)])
+    )(*flags, *counts, *lows, *grads, *([before] if chained else []), *extra)
+
+
+def crossed(mask):
+    return (mask & ~3) | ((mask & 1) << 1) | ((mask & 2) >> 1)
+
+
+def flip(value, mask):
+    rows, dims = lax.axis_size("rows"), lax.axis_size("dims")
+    pairs = [
+        (row * dims + dim, (row ^ (crossed(mask) if dim % 2 else mask)) * dims + dim)
+        for row in range(rows)
+        for dim in range(dims)
+    ]
+    return lax.ppermute(value, ("rows", "dims"), pairs)
+
+
+def flip_dims(value, mask):
+    pairs = [(index, index ^ mask) for index in range(lax.axis_size("dims"))]
+    return lax.ppermute(value, "dims", pairs)
 
 
 def plan(peers):
@@ -296,6 +340,7 @@
     stages = len(bits)
     passes = [phases[0], blocks[0]]
     peers = lax.axis_size("rows")
+    now = len(phases[1]) // 2 if stages > 2 else len(passes[1]) // 2
 
     pieces = [grad_pooled[None]]
     homes = [(0, (0, 0))]
@@ -310,61 +355,68 @@
         )
         pieces.append(piece)
 
-    arrived(flip(pieces[0], "rows", gather_bits[0]), gather_bits[0])
+    arrived(flip(pieces[0], gather_bits[0]), gather_bits[0])
     counts0, halves, low0, flag0, *held = count_call(
-        passes[0], (send_count[None], row, sample, weight, table), pieces[0], peers
+        passes[0], len(passes[0]) // 2, (send_count[None], row, sample, weight, table), pieces[0], peers
     )
     pieces[0] = held.pop()
     halves, pieces[1] = lax.optimization_barrier((halves, pieces[1]))
     sent = len(homes)
-    message = flip(jnp.concatenate(gathered() + [halves]), "rows", bits[0])
+    message = flip(jnp.concatenate(gathered() + [halves]), bits[0])
     arrived(message, gather_bits[1])
     known = {mask for mask, _ in homes}
-    counts1, partial1, low1, flag1 = count_call(passes[1], tuple(held), None, peers)
+    counts1, partial1, low1, flag1 = count_call(passes[1], now, tuple(held), None, peers)
     partial1, message = lax.optimization_barrier((partial1, message))
     pieces[-1] = message
     half = len(passes[0])
-    total = partial1 + (
-        message[sent : sent + half].astype(jnp.float32)
-        + message[sent + half :].astype(jnp.float32)
-    )
+    add = message[sent : sent + half].astype(jnp.float32) + message[sent + half :].astype(jnp.float32)
+    held_back = 2 * now
+    total = (partial1 + add)[:held_back]
+
+    flags, counts, lows = [flag0, flag1], [counts0, counts1], [low0, low1]
+    row_grad = None
     for stage in range(1, stages):
         take = len(phases[stage])
         if stage + 1 < stages:
             arrived(
-                flip(jnp.concatenate(gathered()), "rows", gather_bits[stage + 1]),
+                flip(jnp.concatenate(gathered()), gather_bits[stage + 1]),
                 gather_bits[stage + 1],
             )
-        incoming = flip(total[:take], "rows", bits[stage])
+        incoming = flip(total[:take], bits[stage])
         total = total[take:]
+        if stage == 1:
+            spots = dict(homes)
+            early, late = [], []
+            for part, masks in enumerate(passes):
+                for pair in range(len(masks) // 2):
+                    two = masks[2 * pair : 2 * pair + 2]
+                    (early if set(two) <= known else late).append((part, pair, two))
+            if held_back < len(passes[1]):
+                terms = [(part, pair, *(spots[mask] for mask in two)) for part, pair, two in early]
+                used = 1 + max(home[0] for term in terms for home in term[2:])
+                row_grad, rest = grad_call(
+                    terms, flags, counts, lows, pieces[:used], None, False,
+                    now, (held[4], partial1),
+                )
+                total = rest + add[held_back:]
+            else:
+                late = early + late
         if stage < stages - 1:
             total = total + incoming
 
-    flags, counts, lows = [flag0, flag1], [counts0, counts1], [low0, low1]
     spots = dict(homes)
-    early, late = [], []
-    for part, masks in enumerate(passes):
-        for pair in range(len(masks) // 2):
-            two = masks[2 * pair : 2 * pair + 2]
-            term = (part, pair, spots[two[0]], spots[two[1]])
-            (early if set(two) <= known else late).append(term)
-    row_grad = None
-    if early and late:
-        used = 1 + max(home[0] for term in early for home in term[2:])
-        (row_grad,) = grad_call(early, flags, counts, lows, pieces[:used], None, False)
-    else:
-        late = early + late
-    row_grad, square = grad_call(late, flags, counts, lows, pieces, row_grad, True)
+    terms = [(part, pair, *(spots[mask] for mask in two)) for part, pair, two in late]
+    row_grad, square = grad_call(terms, flags, counts, lows, pieces, row_grad, True)
     return (total, incoming), row_grad, square
 
 
 def share(square):
-    terms = [square]
-    mask = lax.axis_size("dims") // 2
-    while mask >= 1:
-        terms = terms + [flip(term, "dims", mask) for term in terms]
-        mask //= 2
-    return terms
+    size = lax.axis_size("dims")
+    mask = 1
+    while 2 * mask < size:
+        square = square + flip_dims(square, mask)
+        mask *= 2
+    return [square, flip_dims(square, mask)] if size > 1 else [square]
 
 
 def update_kernel(*refs, count, block):
@@ -377,11 +429,10 @@
     row_local = grad_ref.shape[1]
     for index, start in enumerate(range(0, row_local, block)):
         rows = slice(start, start + block)
-        sums = [term[:, rows] for term in terms]
-        while len(sums) > 1:
-            half = len(sums) // 2
-            sums = [sums[place] + sums[place + half] for place in range(half)]
-        total = accum_ref[:, rows] + sums[0] / D
+        squares = terms[0][:, rows]
+        for term in terms[1:]:
+            squares = squares + term[:, rows]
+        total = accum_ref[:, rows] + squares / D
         total_ref[:, rows] = total
         scale = step_size / jnp.sqrt(total)
         new_ref[:, rows] = (

time: 29.1 us -> 29.3 us (level)
  starting transfers between devices: 9.98 us -> 10.4 us
    ppermute x8 -> x7, starting transfers between devices: 9.98 us -> 10.4 us  [the longest x5 8.8 us: flip(): return lax.ppermute(value, ('rows', 'dims'), pairs)]
    pallas_call x2, Pallas kernels: 9.4 us -> 9.01 us  [count_call(): pl.pallas_call(functools.partial(count_kernel, first=first, masks=masks,...]
    pallas_call x2, Pallas kernels: 3.05 us -> 3.41 us  [grad_call(): pl.pallas_call(functools.partial(grad_kernel, terms=terms, pool=pool, par...]
    ppermute x8 -> x7, waiting for transfers between devices: 4.59 us -> 4.36 us  [the longest x5 4.1 us: flip(): return lax.ppermute(value, ('rows', 'dims'), pairs)]
  transfers between devices with their start and end apart: 8 -> 7, of which waited for: 4 -> 4; matrix products, arithmetic and copies ran while one was open for 0% -> 0% of each run, Pallas kernels for 43% -> 37%
where the time goes in v4:
time: 29.3 us; the launch traced here: 29.1 us
  Pallas kernels  13.3 us (45%)
  starting transfers between devices  10.4 us (35%)
  waiting for transfers between devices  4.36 us (15%)
  between operations  0.91 us (3%)
    pallas_call x2, Pallas kernels, count_call(): pl.pallas_call(functools.partial(count_kernel, first=first, masks=masks,...  9.01 us
    ppermute x5, starting transfers between devices, flip(): return lax.ppermute(value, ('rows', 'dims'), pairs)  8.8 us
    ppermute x5, waiting for transfers between devices, flip(): return lax.ppermute(value, ('rows', 'dims'), pairs)  4.1 us
    pallas_call x2, Pallas kernels, grad_call(): pl.pallas_call(functools.partial(grad_kernel, terms=terms, pool=pool, par...  3.41 us
    ppermute x2, starting transfers between devices, flip_dims(): return lax.ppermute(value, 'dims', pairs)  1.63 us
    pallas_call x1, Pallas kernels, update(): pl.pallas_call(functools.partial(update_kernel, count=len(terms), block=b...  0.9 us
  transfers between devices with their start and end apart: 7, of which 4 were waited for; matrix products, arithmetic and copies ran while one was open for 0% of the time, Pallas kernels for 37%

profile of v4, /device:TPU:0, one launch (start us, length us, event | category | flops | bytes accessed | tf_op | source)
XLA Modules:
  0.0 29.1 jit_solution(13666670488088259263)
XLA Ops:
  0.6 4.1 %collective-permute-start = (bf16[1,64,128]{2,1,0:T(8,128)(2,1)}, bf16[1,64,128]{2,1,0:T(8,128)(2,1)S(1)}, u32[]{:S(2)}, u32[]{:S(2)}) collective-permute-start(bf16[1,64,128]{2,1,0:T(8,128)(2,1)} %refs_5_.1), channel_id=1, source_target_pairs={{0,16},{1,17},{2,18},{3,19},{4,20},{5,21},{6,22},{7,23},{8,24},{9,... | collective-permute-start | bytes 49160 | tf_op jit(solution)/shard_map/ppermute | solution.py:316
  4.8 5.1 %counts.2 = (bf16[2,4096,256]{2,1,0:T(8,128)(2,1)S(1)}, bf16[8,64,128]{2,1,0:T(8,128)(2,1)S(1)}, bf16[4,4096,128]{2,1,0:T(8,128)(2,1)S(1)}, f32[16,128]{1,0:T(8,...) custom-call(s32[1,8]{1,0:T(1,128)} %bitcast.11, ...), custom_call_target="tpu_custom_call" | custom-call | tf_op jit(solution)/shard_map/counts/pallas_call | solution.py:184
  9.8 0.0 collective-permute-done.refs_7_
  9.9 1.6 %collective-permute-start.1 = (bf16[10,64,128]{2,1,0:T(8,128)(2,1)S(1)}, bf16[10,64,128]{2,1,0:T(8,128)(2,1)S(1)}, u32[]{:S(2)}, u32[]{:S(2)}) collective-permute-start(bf16[10,64,128]{2,1,0:T(8,128)(2,1)S(1)} %pad_maximum_fusion), channel_id=1, source_target_pairs={{0,4},{1,9},{2,6},{3,11},{4,0},{5,13},{6,2},{7,15},{8,12},{9,1},{1... | collective-permute-start | bytes 491528 | tf_op jit(solution)/shard_map/ppermute | solution.py:316
  11.5 3.9 %counts.3 = (bf16[2,4096,256]{2,1,0:T(8,128)(2,1)S(1)}, f32[4,64,128]{2,1,0:T(8,128)S(1)}, bf16[4,4096,128]{2,1,0:T(8,128)(2,1)S(1)}, f32[16,128]{1,0:T(8,128)S(1)}) custom-call(s32[1,8]{1,0:T(1,128)S(1)} %get-tuple-element.29.refs_0_, s32[8,1280]{1,0:T(8,128)S(1)} %get-tuple-element.30.refs_1_, s32[8,1280]{1,0:T(8,128)S(1)} %get-tuple-element.31.refs_2_, ...), custom_call_target="tpu_custom_call" | custom-call | tf_op jit(solution)/shard_map/counts/pallas_call | solution.py:184
  15.4 0.0 collective-permute-done.1.refs_8_
  15.5 1.1 %collective-permute-start.5 = (f32[2,64,128]{2,1,0:T(8,128)S(1)}, f32[2,64,128]{2,1,0:T(8,128)S(1)}, u32[]{:S(2)}, u32[]{:S(2)}) collective-permute-start(f32[2,64,128]{2,1,0:T(8,128)S(1)} %slice_add_fusion), channel_id=1, source_target_pairs={{0,8},{1,5},{2,10},{3,7},{4,12},{5,1},{6,14},{7,3},{8,0},{9,13},{1... | collective-permute-start | bytes 196616 | tf_op jit(solution)/shard_map/ppermute | solution.py:316
  16.6 1.1 %collective-permute-start.2 = (bf16[4,64,128]{2,1,0:T(8,128)(2,1)S(1)}, bf16[4,64,128]{2,1,0:T(8,128)(2,1)S(1)}, u32[]{:S(2)}, u32[]{:S(2)}) collective-permute-start(bf16[4,64,128]{2,1,0:T(8,128)(2,1)S(1)} %pad_maximum_fusion.1), channel_id=1, source_target_pairs={{0,8},{1,5},{2,10},{3,7},{4,12},{5,1},{6,14},{7,3},{8,0},{9,13},{1... | collective-permute-start | bytes 196616 | tf_op jit(solution)/shard_map/ppermute | solution.py:316
  17.7 1.9 %grads.2 = (f32[64,4096]{1,0:T(8,128)S(1)}, f32[2,64,128]{2,1,0:T(8,128)S(1)}) custom-call(f32[16,128]{1,0:T(8,128)S(1)} %get-tuple-element.28.refs_0_, f32[16,128]{1,0:T(8,128)S(1)} %get-tuple-element.34.refs_1_, bf16[2,4096,256]{2,1,0:T(8,128)(2,1)S(1)} %get-tuple-element.35.refs_2_, bf16[2,4096,256]{2,1,0:T(8,128)(2,1)S(1)} %get-tuple-element.36.refs_3_, ...), custom_call_target="tpu_custom_call" | custom-call | tf_op jit(solution)/shard_map/grads/pallas_call | solution.py:291
  19.5 0.3 collective-permute-done.5
  19.8 1.1 %collective-permute-done.2.refs_9_ = bf16[4,64,128]{2,1,0:T(8,128)(2,1)S(1)} collective-permute-done((bf16[4,64,128]{2,1,0:T(8,128)(2,1)S(1)}, bf16[4,64,128]{2,1,0:T(8,128)(2,1)S(1)}, u32[]{:S(2)}, u32[]{:S(2)}) %collective-permute-start.2) | collective-permute-done | bytes 65568 | tf_op jit(solution)/shard_map/ppermute | solution.py:316
  20.9 0.0 copy-start
  20.9 0.0 copy-start.1
  20.9 1.5 %grads.3 = (f32[64,4096]{1,0:T(8,128)S(1)}, f32[1,4096]{1,0:T(1,128)S(1)}) custom-call(f32[16,128]{1,0:T(8,128)S(1)} %get-tuple-element.28.refs_0_, f32[16,128]{1,0:T(8,128)S(1)} %get-tuple-element.34.refs_1_, bf16[2,4096,256]{2,1,0:T(8,128)(2,1)S(1)} %get-tuple-element.35.refs_2_, bf16[2,4096,256]{2,1,0:T(8,128)(2,1)S(1)} %get-tuple-element.36.refs_3_, ...), custom_call_target="tpu_custom_call" | custom-call | tf_op jit(solution)/shard_map/grads/pallas_call | solution.py:291
  22.5 0.1 collective-permute-start.3
  22.6 0.9 %collective-permute-start.6 = (f32[1,64,128]{2,1,0:T(8,128)S(1)}, f32[1,64,128]{2,1,0:T(8,128)S(1)}, u32[]{:S(2)}, u32[]{:S(2)}) collective-permute-start(f32[1,64,128]{2,1,0:T(8,128)S(1)} %get-tuple-element.53), channel_id=1, source_target_pairs={{0,16},{1,17},{2,18},{3,19},{4,20},{5,21},{6,22},{7,23},{8,24},{9,... | collective-permute-start | bytes 98312 | tf_op jit(solution)/shard_map/ppermute | solution.py:316
  23.5 0.3 collective-permute-done.3
  23.8 1.6 %collective-permute-start.4 = (f32[1,4096]{1,0:T(1,128)S(1)}, f32[1,4096]{1,0:T(1,128)S(1)}, u32[]{:S(2)}, u32[]{:S(2)}) collective-permute-start(f32[1,4096]{1,0:T(1,128)S(1)} %add.15.refs_0_), channel_id=1, source_target_pairs={{0,2},{1,3},{2,0},{3,1},{4,6},{5,7},{6,4},{7,5},{8,10},{9,11},{10,... | collective-permute-start | bytes 49160 | tf_op jit(solution)/shard_map/ppermute | solution.py:321
  25.3 2.7 %collective-permute-done.6.refs_6_ = f32[1,64,128]{2,1,0:T(8,128)S(1)} collective-permute-done((f32[1,64,128]{2,1,0:T(8,128)S(1)}, f32[1,64,128]{2,1,0:T(8,128)S(1)}, u32[]{:S(2)}, u32[]{:S(2)}) %collective-permute-start.6) | collective-permute-done | bytes 32800 | tf_op jit(solution)/shard_map/ppermute | solution.py:316
  28.0 0.0 collective-permute-done.4.refs_1_
  28.0 0.0 copy-done
  28.0 0.0 copy-done.1
  28.0 0.9 %update.1 = (f32[1,64,128]{2,1,0:T(8,128)}, bf16[64,4096]{1,0:T(8,128)(2,1)}, f32[1,4096]{1,0:T(1,128)}) custom-call(f32[1,4096]{1,0:T(1,128)S(1)} %add.15.refs_0_, f32[1,4096]{1,0:T(1,128)S(1)} %collective-permute-done.4.refs_1_, f32[1,4096]{1,0:T(1,128)S(1)} %copy-done.1, bf16[64,4096]{1,0:T(8,128)(2,1)S(1)} %bitcast.7, ...), custom_call_target="tpu_custom_call" | custom-call | tf_op jit(solution)/shard_map/update/pallas_call | solution.py:460
  (8 shorter events, 0.1 us)
Async XLA Ops:
  0.6 9.2 %collective-permute-start = (bf16[1,64,128]{2,1,0:T(8,128)(2,1)}, bf16[1,64,128]{2,1,0:T(8,128)(2,1)S(1)}, u32[]{:S(2)}, u32[]{:S(2)}) collective-permute-start(bf16[1,64,128]{2,1,0:T(8,128)(2,1)} %refs_5_.1), channel_id=1, source_target_pairs={{0,16},{1,17},{2,18},{3,19},{4,20},{5,21},{6,22},{7,23},{8,24},{9,... | collective-permute-start | bytes 49160 | tf_op jit(solution)/shard_map/ppermute | solution.py:316
  9.9 5.6 %collective-permute-start.1 = (bf16[10,64,128]{2,1,0:T(8,128)(2,1)S(1)}, bf16[10,64,128]{2,1,0:T(8,128)(2,1)S(1)}, u32[]{:S(2)}, u32[]{:S(2)}) collective-permute-start(bf16[10,64,128]{2,1,0:T(8,128)(2,1)S(1)} %pad_maximum_fusion), channel_id=1, source_target_pairs={{0,4},{1,9},{2,6},{3,11},{4,0},{5,13},{6,2},{7,15},{8,12},{9,1},{1... | collective-permute-start | bytes 491528 | tf_op jit(solution)/shard_map/ppermute | solution.py:316
  15.5 4.3 %collective-permute-start.5 = (f32[2,64,128]{2,1,0:T(8,128)S(1)}, f32[2,64,128]{2,1,0:T(8,128)S(1)}, u32[]{:S(2)}, u32[]{:S(2)}) collective-permute-start(f32[2,64,128]{2,1,0:T(8,128)S(1)} %slice_add_fusion), channel_id=1, source_target_pairs={{0,8},{1,5},{2,10},{3,7},{4,12},{5,1},{6,14},{7,3},{8,0},{9,13},{1... | collective-permute-start | bytes 196616 | tf_op jit(solution)/shard_map/ppermute | solution.py:316
  16.6 4.3 %collective-permute-start.2 = (bf16[4,64,128]{2,1,0:T(8,128)(2,1)S(1)}, bf16[4,64,128]{2,1,0:T(8,128)(2,1)S(1)}, u32[]{:S(2)}, u32[]{:S(2)}) collective-permute-start(bf16[4,64,128]{2,1,0:T(8,128)(2,1)S(1)} %pad_maximum_fusion.1), channel_id=1, source_target_pairs={{0,8},{1,5},{2,10},{3,7},{4,12},{5,1},{6,14},{7,3},{8,0},{9,13},{1... | collective-permute-start | bytes 196616 | tf_op jit(solution)/shard_map/ppermute | solution.py:316
  20.9 7.1 %copy-start = (bf16[1,64,4096]{2,1,0:T(8,128)(2,1)S(1)}, bf16[1,64,4096]{2,1,0:T(8,128)(2,1)}, u32[]{:S(2)}) copy-start(bf16[1,64,4096]{2,1,0:T(8,128)(2,1)} %param.7) | copy-start | bytes 1572868
  20.9 7.1 %copy-start.1 = (f32[1,4096]{1,0:T(1,128)S(1)}, f32[1,4096]{1,0:T(1,128)}, u32[]{:S(2)}) copy-start(f32[1,4096]{1,0:T(1,128)} %refs_2_.1) | copy-start | bytes 49156
  22.5 1.2 %collective-permute-start.3 = (f32[1,4096]{1,0:T(1,128)S(1)}, f32[1,4096]{1,0:T(1,128)S(1)}, u32[]{:S(2)}, u32[]{:S(2)}) collective-permute-start(f32[1,4096]{1,0:T(1,128)S(1)} %get-tuple-element.47), channel_id=1, source_target_pairs={{0,1},{1,0},{2,3},{3,2},{4,5},{5,4},{6,7},{7,6},{8,9},{9,8},{10,11... | collective-permute-start | bytes 49160 | tf_op jit(solution)/shard_map/ppermute | solution.py:321
  22.6 5.5 %collective-permute-start.6 = (f32[1,64,128]{2,1,0:T(8,128)S(1)}, f32[1,64,128]{2,1,0:T(8,128)S(1)}, u32[]{:S(2)}, u32[]{:S(2)}) collective-permute-start(f32[1,64,128]{2,1,0:T(8,128)S(1)} %get-tuple-element.53), channel_id=1, source_target_pairs={{0,16},{1,17},{2,18},{3,19},{4,20},{5,21},{6,22},{7,23},{8,24},{9,... | collective-permute-start | bytes 98312 | tf_op jit(solution)/shard_map/ppermute | solution.py:316
  23.8 4.3 %collective-permute-start.4 = (f32[1,4096]{1,0:T(1,128)S(1)}, f32[1,4096]{1,0:T(1,128)S(1)}, u32[]{:S(2)}, u32[]{:S(2)}) collective-permute-start(f32[1,4096]{1,0:T(1,128)S(1)} %add.15.refs_0_), channel_id=1, source_target_pairs={{0,2},{1,3},{2,0},{3,1},{4,6},{5,7},{6,4},{7,5},{8,10},{9,11},{10,... | collective-permute-start | bytes 49160 | tf_op jit(solution)/shard_map/ppermute | solution.py:321

commit v5 on v4

--- a/solution.py
+++ b/solution.py
@@ -411,12 +411,12 @@
 
 
 def share(square):
-    size = lax.axis_size("dims")
-    mask = 1
-    while 2 * mask < size:
-        square = square + flip_dims(square, mask)
-        mask *= 2
-    return [square, flip_dims(square, mask)] if size > 1 else [square]
+    terms = [square]
+    mask = lax.axis_size("dims") // 2
+    while mask >= 1:
+        terms = terms + [flip_dims(term, mask) for term in terms]
+        mask //= 2
+    return terms
 
 
 def update_kernel(*refs, count, block):
@@ -429,9 +429,11 @@
     row_local = grad_ref.shape[1]
     for index, start in enumerate(range(0, row_local, block)):
         rows = slice(start, start + block)
-        squares = terms[0][:, rows]
-        for term in terms[1:]:
-            squares = squares + term[:, rows]
+        sums = [term[:, rows] for term in terms]
+        while len(sums) > 1:
+            half = len(sums) // 2
+            sums = [sums[place] + sums[place + half] for place in range(half)]
+        squares = sums[0]
         total = accum_ref[:, rows] + squares / D
         total_ref[:, rows] = total
         scale = step_size / jnp.sqrt(total)

time: 29.3 us -> 30.1 us (1.027)
  waiting for transfers between devices: 4.36 us -> 5.33 us
    ppermute x2 -> x3, waiting for transfers between devices: 0.26 us -> 1.4 us  [flip_dims(): return lax.ppermute(value, 'dims', pairs)]
    ppermute x2 -> x3, starting transfers between devices: 1.63 us -> 1.56 us  [flip_dims(): return lax.ppermute(value, 'dims', pairs)]
  transfers between devices with their start and end apart: 7 -> 8, of which waited for: 4 -> 4; matrix products, arithmetic and copies ran while one was open for 0% -> 0% of each run, Pallas kernels for 37% -> 36%
where the time goes in v5:
time: 30.1 us; the launch traced here: 29.9 us
  Pallas kernels  13.3 us (44%)
  starting transfers between devices  10.3 us (34%)
  waiting for transfers between devices  5.33 us (18%)
  between operations  0.9 us (3%)
    pallas_call x2, Pallas kernels, count_call(): pl.pallas_call(functools.partial(count_kernel, first=first, masks=masks,...  9.01 us
    ppermute x5, starting transfers between devices, flip(): return lax.ppermute(value, ('rows', 'dims'), pairs)  8.73 us
    ppermute x5, waiting for transfers between devices, flip(): return lax.ppermute(value, ('rows', 'dims'), pairs)  3.93 us
    pallas_call x2, Pallas kernels, grad_call(): pl.pallas_call(functools.partial(grad_kernel, terms=terms, pool=pool, par...  3.41 us
    ppermute x3, starting transfers between devices, flip_dims(): return lax.ppermute(value, 'dims', pairs)  1.56 us
    ppermute x3, waiting for transfers between devices, flip_dims(): return lax.ppermute(value, 'dims', pairs)  1.4 us
    pallas_call x1, Pallas kernels, update(): pl.pallas_call(functools.partial(update_kernel, count=len(terms), block=b...  0.9 us
  transfers between devices with their start and end apart: 8, of which 4 were waited for; matrix products, arithmetic and copies ran while one was open for 0% of the time, Pallas kernels for 36%

profile of v5, /device:TPU:0, one launch (start us, length us, event | category | flops | bytes accessed | tf_op | source)
XLA Modules:
  0.0 29.9 jit_solution(2261389758876345890)
XLA Ops:
  0.6 4.1 %collective-permute-start = (bf16[1,64,128]{2,1,0:T(8,128)(2,1)}, bf16[1,64,128]{2,1,0:T(8,128)(2,1)S(1)}, u32[]{:S(2)}, u32[]{:S(2)}) collective-permute-start(bf16[1,64,128]{2,1,0:T(8,128)(2,1)} %refs_5_.1), channel_id=1, source_target_pairs={{0,16},{1,17},{2,18},{3,19},{4,20},{5,21},{6,22},{7,23},{8,24},{9,... | collective-permute-start | bytes 49160 | tf_op jit(solution)/shard_map/ppermute | solution.py:316
  4.8 5.1 %counts.2 = (bf16[2,4096,256]{2,1,0:T(8,128)(2,1)S(1)}, bf16[8,64,128]{2,1,0:T(8,128)(2,1)S(1)}, bf16[4,4096,128]{2,1,0:T(8,128)(2,1)S(1)}, f32[16,128]{1,0:T(8,...) custom-call(s32[1,8]{1,0:T(1,128)} %bitcast.11, ...), custom_call_target="tpu_custom_call" | custom-call | tf_op jit(solution)/shard_map/counts/pallas_call | solution.py:184
  9.8 0.0 collective-permute-done.refs_7_
  9.9 1.6 %collective-permute-start.1 = (bf16[10,64,128]{2,1,0:T(8,128)(2,1)S(1)}, bf16[10,64,128]{2,1,0:T(8,128)(2,1)S(1)}, u32[]{:S(2)}, u32[]{:S(2)}) collective-permute-start(bf16[10,64,128]{2,1,0:T(8,128)(2,1)S(1)} %pad_maximum_fusion), channel_id=1, source_target_pairs={{0,4},{1,9},{2,6},{3,11},{4,0},{5,13},{6,2},{7,15},{8,12},{9,1},{1... | collective-permute-start | bytes 491528 | tf_op jit(solution)/shard_map/ppermute | solution.py:316
  11.5 3.9 %counts.3 = (bf16[2,4096,256]{2,1,0:T(8,128)(2,1)S(1)}, f32[4,64,128]{2,1,0:T(8,128)S(1)}, bf16[4,4096,128]{2,1,0:T(8,128)(2,1)S(1)}, f32[16,128]{1,0:T(8,128)S(1)}) custom-call(s32[1,8]{1,0:T(1,128)S(1)} %get-tuple-element.29.refs_0_, s32[8,1280]{1,0:T(8,128)S(1)} %get-tuple-element.30.refs_1_, s32[8,1280]{1,0:T(8,128)S(1)} %get-tuple-element.31.refs_2_, ...), custom_call_target="tpu_custom_call" | custom-call | tf_op jit(solution)/shard_map/counts/pallas_call | solution.py:184
  15.4 0.0 collective-permute-done.1.refs_8_
  15.5 1.1 %collective-permute-start.6 = (f32[2,64,128]{2,1,0:T(8,128)S(1)}, f32[2,64,128]{2,1,0:T(8,128)S(1)}, u32[]{:S(2)}, u32[]{:S(2)}) collective-permute-start(f32[2,64,128]{2,1,0:T(8,128)S(1)} %slice_add_fusion), channel_id=1, source_target_pairs={{0,8},{1,5},{2,10},{3,7},{4,12},{5,1},{6,14},{7,3},{8,0},{9,13},{1... | collective-permute-start | bytes 196616 | tf_op jit(solution)/shard_map/ppermute | solution.py:316
  16.6 1.1 %collective-permute-start.2 = (bf16[4,64,128]{2,1,0:T(8,128)(2,1)S(1)}, bf16[4,64,128]{2,1,0:T(8,128)(2,1)S(1)}, u32[]{:S(2)}, u32[]{:S(2)}) collective-permute-start(bf16[4,64,128]{2,1,0:T(8,128)(2,1)S(1)} %pad_maximum_fusion.1), channel_id=1, source_target_pairs={{0,8},{1,5},{2,10},{3,7},{4,12},{5,1},{6,14},{7,3},{8,0},{9,13},{1... | collective-permute-start | bytes 196616 | tf_op jit(solution)/shard_map/ppermute | solution.py:316
  17.7 1.9 %grads.2 = (f32[64,4096]{1,0:T(8,128)S(1)}, f32[2,64,128]{2,1,0:T(8,128)S(1)}) custom-call(f32[16,128]{1,0:T(8,128)S(1)} %get-tuple-element.28.refs_0_, f32[16,128]{1,0:T(8,128)S(1)} %get-tuple-element.34.refs_1_, bf16[2,4096,256]{2,1,0:T(8,128)(2,1)S(1)} %get-tuple-element.35.refs_2_, bf16[2,4096,256]{2,1,0:T(8,128)(2,1)S(1)} %get-tuple-element.36.refs_3_, ...), custom_call_target="tpu_custom_call" | custom-call | tf_op jit(solution)/shard_map/grads/pallas_call | solution.py:291
  19.5 0.3 collective-permute-done.6
  19.8 1.1 %collective-permute-done.2.refs_9_ = bf16[4,64,128]{2,1,0:T(8,128)(2,1)S(1)} collective-permute-done((bf16[4,64,128]{2,1,0:T(8,128)(2,1)S(1)}, bf16[4,64,128]{2,1,0:T(8,128)(2,1)S(1)}, u32[]{:S(2)}, u32[]{:S(2)}) %collective-permute-start.2) | collective-permute-done | bytes 65568 | tf_op jit(solution)/shard_map/ppermute | solution.py:316
  20.9 0.0 copy-start
  20.9 0.0 copy-start.1
  20.9 1.5 %grads.3 = (f32[64,4096]{1,0:T(8,128)S(1)}, f32[1,4096]{1,0:T(1,128)S(1)}) custom-call(f32[16,128]{1,0:T(8,128)S(1)} %get-tuple-element.28.refs_0_, f32[16,128]{1,0:T(8,128)S(1)} %get-tuple-element.34.refs_1_, bf16[2,4096,256]{2,1,0:T(8,128)(2,1)S(1)} %get-tuple-element.35.refs_2_, bf16[2,4096,256]{2,1,0:T(8,128)(2,1)S(1)} %get-tuple-element.36.refs_3_, ...), custom_call_target="tpu_custom_call" | custom-call | tf_op jit(solution)/shard_map/grads/pallas_call | solution.py:291
  22.5 1.6 %collective-permute-start.3 = (f32[1,4096]{1,0:T(1,128)S(1)}, f32[1,4096]{1,0:T(1,128)S(1)}, u32[]{:S(2)}, u32[]{:S(2)}) collective-permute-start(f32[1,4096]{1,0:T(1,128)S(1)} %get-tuple-element.47.refs_0_), channel_id=1, source_target_pairs={{0,2},{1,3},{2,0},{3,1},{4,6},{5,7},{6,4},{7,5},{8,10},{9,11},{10,... | collective-permute-start | bytes 49160 | tf_op jit(solution)/shard_map/ppermute | solution.py:321
  24.0 0.8 %collective-permute-start.7 = (f32[1,64,128]{2,1,0:T(8,128)S(1)}, f32[1,64,128]{2,1,0:T(8,128)S(1)}, u32[]{:S(2)}, u32[]{:S(2)}) collective-permute-start(f32[1,64,128]{2,1,0:T(8,128)S(1)} %get-tuple-element.53), channel_id=1, source_target_pairs={{0,16},{1,17},{2,18},{3,19},{4,20},{5,21},{6,22},{7,23},{8,24},{9,... | collective-permute-start | bytes 98312 | tf_op jit(solution)/shard_map/ppermute | solution.py:316
  24.9 0.0 collective-permute-start.4
  24.9 1.4 %collective-permute-done.3.refs_1_ = f32[1,4096]{1,0:T(1,128)S(1)} collective-permute-done((f32[1,4096]{1,0:T(1,128)S(1)}, f32[1,4096]{1,0:T(1,128)S(1)}, u32[]{:S(2)}, u32[]{:S(2)}) %collective-permute-start.3) | collective-permute-done | bytes 16416 | tf_op jit(solution)/shard_map/ppermute | solution.py:321
  26.3 0.0 collective-permute-start.5
  26.3 0.0 collective-permute-done.4.refs_2_
  26.3 2.6 %collective-permute-done.7.refs_8_ = f32[1,64,128]{2,1,0:T(8,128)S(1)} collective-permute-done((f32[1,64,128]{2,1,0:T(8,128)S(1)}, f32[1,64,128]{2,1,0:T(8,128)S(1)}, u32[]{:S(2)}, u32[]{:S(2)}) %collective-permute-start.7) | collective-permute-done | bytes 32800 | tf_op jit(solution)/shard_map/ppermute | solution.py:316
  28.8 0.0 collective-permute-done.5.refs_3_
  28.9 0.0 copy-done
  28.9 0.0 copy-done.1
  28.9 0.9 %update.1 = (f32[1,64,128]{2,1,0:T(8,128)}, bf16[64,4096]{1,0:T(8,128)(2,1)}, f32[1,4096]{1,0:T(1,128)}) custom-call(f32[1,4096]{1,0:T(1,128)S(1)} %get-tuple-element.47.refs_0_, f32[1,4096]{1,0:T(1,128)S(1)} %collective-permute-done.3.refs_1_, f32[1,4096]{1,0:T(1,128)S(1)} %collective-permute-done.4.refs_2_, f32[1,4096]{1,0:T(1,128)S(1)} %collective-permute-done.5.refs_3_, ...), custom_call_target="tpu_custom_call" | custom-call | tf_op jit(solution)/shard_map/update/pallas_call | solution.py:462
  (7 shorter events, 0.1 us)
Async XLA Ops:
  0.6 9.2 %collective-permute-start = (bf16[1,64,128]{2,1,0:T(8,128)(2,1)}, bf16[1,64,128]{2,1,0:T(8,128)(2,1)S(1)}, u32[]{:S(2)}, u32[]{:S(2)}) collective-permute-start(bf16[1,64,128]{2,1,0:T(8,128)(2,1)} %refs_5_.1), channel_id=1, source_target_pairs={{0,16},{1,17},{2,18},{3,19},{4,20},{5,21},{6,22},{7,23},{8,24},{9,... | collective-permute-start | bytes 49160 | tf_op jit(solution)/shard_map/ppermute | solution.py:316
  9.9 5.6 %collective-permute-start.1 = (bf16[10,64,128]{2,1,0:T(8,128)(2,1)S(1)}, bf16[10,64,128]{2,1,0:T(8,128)(2,1)S(1)}, u32[]{:S(2)}, u32[]{:S(2)}) collective-permute-start(bf16[10,64,128]{2,1,0:T(8,128)(2,1)S(1)} %pad_maximum_fusion), channel_id=1, source_target_pairs={{0,4},{1,9},{2,6},{3,11},{4,0},{5,13},{6,2},{7,15},{8,12},{9,1},{1... | collective-permute-start | bytes 491528 | tf_op jit(solution)/shard_map/ppermute | solution.py:316
  15.5 4.3 %collective-permute-start.6 = (f32[2,64,128]{2,1,0:T(8,128)S(1)}, f32[2,64,128]{2,1,0:T(8,128)S(1)}, u32[]{:S(2)}, u32[]{:S(2)}) collective-permute-start(f32[2,64,128]{2,1,0:T(8,128)S(1)} %slice_add_fusion), channel_id=1, source_target_pairs={{0,8},{1,5},{2,10},{3,7},{4,12},{5,1},{6,14},{7,3},{8,0},{9,13},{1... | collective-permute-start | bytes 196616 | tf_op jit(solution)/shard_map/ppermute | solution.py:316
  16.6 4.3 %collective-permute-start.2 = (bf16[4,64,128]{2,1,0:T(8,128)(2,1)S(1)}, bf16[4,64,128]{2,1,0:T(8,128)(2,1)S(1)}, u32[]{:S(2)}, u32[]{:S(2)}) collective-permute-start(bf16[4,64,128]{2,1,0:T(8,128)(2,1)S(1)} %pad_maximum_fusion.1), channel_id=1, source_target_pairs={{0,8},{1,5},{2,10},{3,7},{4,12},{5,1},{6,14},{7,3},{8,0},{9,13},{1... | collective-permute-start | bytes 196616 | tf_op jit(solution)/shard_map/ppermute | solution.py:316
  20.9 7.9 %copy-start = (bf16[1,64,4096]{2,1,0:T(8,128)(2,1)S(1)}, bf16[1,64,4096]{2,1,0:T(8,128)(2,1)}, u32[]{:S(2)}) copy-start(bf16[1,64,4096]{2,1,0:T(8,128)(2,1)} %param.7) | copy-start | bytes 1572868
  20.9 7.9 %copy-start.1 = (f32[1,4096]{1,0:T(1,128)S(1)}, f32[1,4096]{1,0:T(1,128)}, u32[]{:S(2)}) copy-start(f32[1,4096]{1,0:T(1,128)} %refs_4_.1) | copy-start | bytes 49156
  22.5 3.8 %collective-permute-start.3 = (f32[1,4096]{1,0:T(1,128)S(1)}, f32[1,4096]{1,0:T(1,128)S(1)}, u32[]{:S(2)}, u32[]{:S(2)}) collective-permute-start(f32[1,4096]{1,0:T(1,128)S(1)} %get-tuple-element.47.refs_0_), channel_id=1, source_target_pairs={{0,2},{1,3},{2,0},{3,1},{4,6},{5,7},{6,4},{7,5},{8,10},{9,11},{10,... | collective-permute-start | bytes 49160 | tf_op jit(solution)/shard_map/ppermute | solution.py:321
  24.0 4.8 %collective-permute-start.7 = (f32[1,64,128]{2,1,0:T(8,128)S(1)}, f32[1,64,128]{2,1,0:T(8,128)S(1)}, u32[]{:S(2)}, u32[]{:S(2)}) collective-permute-start(f32[1,64,128]{2,1,0:T(8,128)S(1)} %get-tuple-element.53), channel_id=1, source_target_pairs={{0,16},{1,17},{2,18},{3,19},{4,20},{5,21},{6,22},{7,23},{8,24},{9,... | collective-permute-start | bytes 98312 | tf_op jit(solution)/shard_map/ppermute | solution.py:316
  24.9 1.4 %collective-permute-start.4 = (f32[1,4096]{1,0:T(1,128)S(1)}, f32[1,4096]{1,0:T(1,128)S(1)}, u32[]{:S(2)}, u32[]{:S(2)}) collective-permute-start(f32[1,4096]{1,0:T(1,128)S(1)} %get-tuple-element.47.refs_0_), channel_id=1, source_target_pairs={{0,1},{1,0},{2,3},{3,2},{4,5},{5,4},{6,7},{7,6},{8,9},{9,8},{10,11... | collective-permute-start | bytes 49160 | tf_op jit(solution)/shard_map/ppermute | solution.py:321
  26.3 2.6 %collective-permute-start.5 = (f32[1,4096]{1,0:T(1,128)S(1)}, f32[1,4096]{1,0:T(1,128)S(1)}, u32[]{:S(2)}, u32[]{:S(2)}) collective-permute-start(f32[1,4096]{1,0:T(1,128)S(1)} %collective-permute-done.3.refs_1_), channel_id=1, source_target_pairs={{0,1},{1,0},{2,3},{3,2},{4,5},{5,4},{6,7},{7,6},{8,9},{9,8},{10,11... | collective-permute-start | bytes 49160 | tf_op jit(solution)/shard_map/ppermute | solution.py:321

commit v6 on v5

--- a/solution.py
+++ b/solution.py
@@ -59,17 +59,13 @@
         ]
         for load in loads:
             load.start()
-        _, row_ref, sample_ref, weight_ref, table_ref = held[:5]
-        scalars = pltpu.make_async_copy(sources[0], count_ref, sems.at[6])
+        live_ref, row_ref, sample_ref, weight_ref, table_ref = held[:5]
     else:
-        _, row_ref, sample_ref, weight_ref, table_ref = sources
-        scalars = pltpu.make_async_copy(sources[0], count_ref, sems.at[6])
-    scalars.start()
+        live_ref, row_ref, sample_ref, weight_ref, table_ref = sources
     me = lax.axis_index("rows")
     most_ref[...] = jnp.zeros_like(most_ref)
     for load in loads[:4]:
         load.wait()
-    scalars.wait()
 
     odd = lax.axis_index("dims") % 2
 
@@ -80,10 +76,16 @@
             odd_mask = jnp.where(index == place, crossed(mask), odd_mask)
         return me ^ jnp.where(odd == 1, odd_mask, even_mask)
 
+    lives = live_ref[...].astype(jnp.float32)
+    places = lax.broadcasted_iota(jnp.int32, lives.shape, 1)
+    for index in range(len(masks)):
+        mine = jnp.where(places == owner_of(index), lives, 0.0)
+        count_ref[0, index] = jnp.sum(mine).astype(jnp.int32)
+
     def count_pair(pair, carry):
         for member in range(2):
             owner = owner_of(2 * pair + member)
-            count = count_ref[0, owner]
+            count = count_ref[0, 2 * pair + member]
             row = row_ref[pl.ds(owner, 1), :]
             sample = sample_ref[pl.ds(owner, 1), :]
             weight = weight_ref[pl.ds(owner, 1), :]
@@ -127,7 +129,7 @@
 
         return carry
 
-    lax.fori_loop(0, len(masks) // 2, count_pair, 0)
+    lax.fori_loop(0, len(masks) // 2, count_pair, 0, unroll=True)
 
     most = most_ref[0:16, :]
     for start in range(16, low, 16):
@@ -140,7 +142,7 @@
             owner = owner_of(index)
             counts = factor_product(
                 row_ref[pl.ds(owner, 1), :], sample_ref[pl.ds(owner, 1), :],
-                weight_ref[pl.ds(owner, 1), :], count_ref[0, owner], low, span, row_ref.shape[1],
+                weight_ref[pl.ds(owner, 1), :], count_ref[0, index], low, span, row_ref.shape[1],
             )
             rest = (counts - counts.astype(jnp.bfloat16).astype(jnp.float32)).astype(jnp.bfloat16)
             for part in range(span):
@@ -193,7 +195,7 @@
             pltpu.VMEM((low, LANES), jnp.bfloat16),
             pltpu.VMEM((row_local, LANES), jnp.bfloat16),
             pltpu.VMEM((total, dim_local, LANES), jnp.float32),
-            pltpu.SemaphoreType.DMA((7,)),
+            pltpu.SemaphoreType.DMA((6,)),
         ],
         out_shape=[
             jax.ShapeDtypeStruct((total // 2, row_local, 2 * LANES), jnp.bfloat16),

time: 30.1 us -> 29.7 us (0.987)
  Pallas kernels: 13.3 us -> 12.9 us
    pallas_call x2, Pallas kernels: 9.01 us -> 8.63 us  [count_call(): pl.pallas_call(functools.partial(count_kernel, first=first, masks=masks,...]
  transfers between devices with their start and end apart: 8 -> 8, of which waited for: 4 -> 5; matrix products, arithmetic and copies ran while one was open for 0% -> 0% of each run, Pallas kernels for 36% -> 35%
where the time goes in v6:
time: 29.7 us; the launch traced here: 29.6 us
  Pallas kernels  12.9 us (43%)
  starting transfers between devices  10.6 us (36%)
  waiting for transfers between devices  5.09 us (17%)
  between operations  0.9 us (3%)
    ppermute x5, starting transfers between devices, flip(): return lax.ppermute(value, ('rows', 'dims'), pairs)  8.99 us
    pallas_call x2, Pallas kernels, count_call(): pl.pallas_call(functools.partial(count_kernel, first=first, masks=masks,...  8.63 us
    ppermute x5, waiting for transfers between devices, flip(): return lax.ppermute(value, ('rows', 'dims'), pairs)  3.91 us
    pallas_call x2, Pallas kernels, grad_call(): pl.pallas_call(functools.partial(grad_kernel, terms=terms, pool=pool, par...  3.41 us
    ppermute x3, starting transfers between devices, flip_dims(): return lax.ppermute(value, 'dims', pairs)  1.56 us
    ppermute x3, waiting for transfers between devices, flip_dims(): return lax.ppermute(value, 'dims', pairs)  1.18 us
    pallas_call x1, Pallas kernels, update(): pl.pallas_call(functools.partial(update_kernel, count=len(terms), block=b...  0.9 us
  transfers between devices with their start and end apart: 8, of which 5 were waited for; matrix products, arithmetic and copies ran while one was open for 0% of the time, Pallas kernels for 35%

profile of v6, /device:TPU:0, one launch (start us, length us, event | category | flops | bytes accessed | tf_op | source)
XLA Modules:
  0.0 29.6 jit_solution(13735932173935775007)
XLA Ops:
  0.6 4.1 %collective-permute-start = (bf16[1,64,128]{2,1,0:T(8,128)(2,1)}, bf16[1,64,128]{2,1,0:T(8,128)(2,1)S(1)}, u32[]{:S(2)}, u32[]{:S(2)}) collective-permute-start(bf16[1,64,128]{2,1,0:T(8,128)(2,1)} %refs_5_.1), channel_id=1, source_target_pairs={{0,16},{1,17},{2,18},{3,19},{4,20},{5,21},{6,22},{7,23},{8,24},{9,... | collective-permute-start | bytes 49160 | tf_op jit(solution)/shard_map/ppermute | solution.py:318
  4.8 5.0 %counts.2 = (bf16[2,4096,256]{2,1,0:T(8,128)(2,1)S(1)}, bf16[8,64,128]{2,1,0:T(8,128)(2,1)S(1)}, bf16[4,4096,128]{2,1,0:T(8,128)(2,1)S(1)}, f32[16,128]{1,0:T(8,...) custom-call(s32[1,8]{1,0:T(1,128)} %bitcast.11, ...), custom_call_target="tpu_custom_call" | custom-call | tf_op jit(solution)/shard_map/counts/pallas_call | solution.py:186
  9.7 0.0 collective-permute-done.refs_7_
  9.8 1.6 %collective-permute-start.1 = (bf16[10,64,128]{2,1,0:T(8,128)(2,1)S(1)}, bf16[10,64,128]{2,1,0:T(8,128)(2,1)S(1)}, u32[]{:S(2)}, u32[]{:S(2)}) collective-permute-start(bf16[10,64,128]{2,1,0:T(8,128)(2,1)S(1)} %pad_maximum_fusion), channel_id=1, source_target_pairs={{0,4},{1,9},{2,6},{3,11},{4,0},{5,13},{6,2},{7,15},{8,12},{9,1},{1... | collective-permute-start | bytes 491528 | tf_op jit(solution)/shard_map/ppermute | solution.py:318
  11.4 3.7 %counts.3 = (bf16[2,4096,256]{2,1,0:T(8,128)(2,1)S(1)}, f32[4,64,128]{2,1,0:T(8,128)S(1)}, bf16[4,4096,128]{2,1,0:T(8,128)(2,1)S(1)}, f32[16,128]{1,0:T(8,128)S(1)}) custom-call(s32[1,8]{1,0:T(1,128)S(1)} %get-tuple-element.29.refs_0_, s32[8,1280]{1,0:T(8,128)S(1)} %get-tuple-element.30.refs_1_, s32[8,1280]{1,0:T(8,128)S(1)} %get-tuple-element.31.refs_2_, ...), custom_call_target="tpu_custom_call" | custom-call | tf_op jit(solution)/shard_map/counts/pallas_call | solution.py:186
  15.0 0.1 collective-permute-done.1.refs_8_
  15.2 1.0 %collective-permute-start.6 = (f32[2,64,128]{2,1,0:T(8,128)S(1)}, f32[2,64,128]{2,1,0:T(8,128)S(1)}, u32[]{:S(2)}, u32[]{:S(2)}) collective-permute-start(f32[2,64,128]{2,1,0:T(8,128)S(1)} %slice_add_fusion), channel_id=1, source_target_pairs={{0,8},{1,5},{2,10},{3,7},{4,12},{5,1},{6,14},{7,3},{8,0},{9,13},{1... | collective-permute-start | bytes 196616 | tf_op jit(solution)/shard_map/ppermute | solution.py:318
  16.2 1.1 %collective-permute-start.2 = (bf16[4,64,128]{2,1,0:T(8,128)(2,1)S(1)}, bf16[4,64,128]{2,1,0:T(8,128)(2,1)S(1)}, u32[]{:S(2)}, u32[]{:S(2)}) collective-permute-start(bf16[4,64,128]{2,1,0:T(8,128)(2,1)S(1)} %pad_maximum_fusion.1), channel_id=1, source_target_pairs={{0,8},{1,5},{2,10},{3,7},{4,12},{5,1},{6,14},{7,3},{8,0},{9,13},{1... | collective-permute-start | bytes 196616 | tf_op jit(solution)/shard_map/ppermute | solution.py:318
  17.4 1.9 %grads.2 = (f32[64,4096]{1,0:T(8,128)S(1)}, f32[2,64,128]{2,1,0:T(8,128)S(1)}) custom-call(f32[16,128]{1,0:T(8,128)S(1)} %get-tuple-element.28.refs_0_, f32[16,128]{1,0:T(8,128)S(1)} %get-tuple-element.34.refs_1_, bf16[2,4096,256]{2,1,0:T(8,128)(2,1)S(1)} %get-tuple-element.35.refs_2_, bf16[2,4096,256]{2,1,0:T(8,128)(2,1)S(1)} %get-tuple-element.36.refs_3_, ...), custom_call_target="tpu_custom_call" | custom-call | tf_op jit(solution)/shard_map/grads/pallas_call | solution.py:293
  19.2 0.3 collective-permute-done.6
  19.6 1.0 %collective-permute-done.2.refs_9_ = bf16[4,64,128]{2,1,0:T(8,128)(2,1)S(1)} collective-permute-done((bf16[4,64,128]{2,1,0:T(8,128)(2,1)S(1)}, bf16[4,64,128]{2,1,0:T(8,128)(2,1)S(1)}, u32[]{:S(2)}, u32[]{:S(2)}) %collective-permute-start.2) | collective-permute-done | bytes 65568 | tf_op jit(solution)/shard_map/ppermute | solution.py:318
  20.6 0.0 copy-start
  20.6 0.0 copy-start.1
  20.6 1.5 %grads.3 = (f32[64,4096]{1,0:T(8,128)S(1)}, f32[1,4096]{1,0:T(1,128)S(1)}) custom-call(f32[16,128]{1,0:T(8,128)S(1)} %get-tuple-element.28.refs_0_, f32[16,128]{1,0:T(8,128)S(1)} %get-tuple-element.34.refs_1_, bf16[2,4096,256]{2,1,0:T(8,128)(2,1)S(1)} %get-tuple-element.35.refs_2_, bf16[2,4096,256]{2,1,0:T(8,128)(2,1)S(1)} %get-tuple-element.36.refs_3_, ...), custom_call_target="tpu_custom_call" | custom-call | tf_op jit(solution)/shard_map/grads/pallas_call | solution.py:293
  22.1 1.6 %collective-permute-start.3 = (f32[1,4096]{1,0:T(1,128)S(1)}, f32[1,4096]{1,0:T(1,128)S(1)}, u32[]{:S(2)}, u32[]{:S(2)}) collective-permute-start(f32[1,4096]{1,0:T(1,128)S(1)} %get-tuple-element.47.refs_0_), channel_id=1, source_target_pairs={{0,2},{1,3},{2,0},{3,1},{4,6},{5,7},{6,4},{7,5},{8,10},{9,11},{10,... | collective-permute-start | bytes 49160 | tf_op jit(solution)/shard_map/ppermute | solution.py:323
  23.7 1.1 %collective-permute-start.7 = (f32[1,64,128]{2,1,0:T(8,128)S(1)}, f32[1,64,128]{2,1,0:T(8,128)S(1)}, u32[]{:S(2)}, u32[]{:S(2)}) collective-permute-start(f32[1,64,128]{2,1,0:T(8,128)S(1)} %get-tuple-element.53), channel_id=1, source_target_pairs={{0,16},{1,17},{2,18},{3,19},{4,20},{5,21},{6,22},{7,23},{8,24},{9,... | collective-permute-start | bytes 98312 | tf_op jit(solution)/shard_map/ppermute | solution.py:318
  24.8 0.0 collective-permute-start.4
  24.8 1.1 %collective-permute-done.3.refs_1_ = f32[1,4096]{1,0:T(1,128)S(1)} collective-permute-done((f32[1,4096]{1,0:T(1,128)S(1)}, f32[1,4096]{1,0:T(1,128)S(1)}, u32[]{:S(2)}, u32[]{:S(2)}) %collective-permute-start.3) | collective-permute-done | bytes 16416 | tf_op jit(solution)/shard_map/ppermute | solution.py:323
  25.9 0.0 collective-permute-start.5
  25.9 0.0 collective-permute-done.4.refs_2_
  26.0 2.5 %collective-permute-done.7.refs_8_ = f32[1,64,128]{2,1,0:T(8,128)S(1)} collective-permute-done((f32[1,64,128]{2,1,0:T(8,128)S(1)}, f32[1,64,128]{2,1,0:T(8,128)S(1)}, u32[]{:S(2)}, u32[]{:S(2)}) %collective-permute-start.7) | collective-permute-done | bytes 32800 | tf_op jit(solution)/shard_map/ppermute | solution.py:318
  28.5 0.0 collective-permute-done.5.refs_3_
  28.5 0.0 copy-done
  28.5 0.0 copy-done.1
  28.5 0.9 %update.1 = (f32[1,64,128]{2,1,0:T(8,128)}, bf16[64,4096]{1,0:T(8,128)(2,1)}, f32[1,4096]{1,0:T(1,128)}) custom-call(f32[1,4096]{1,0:T(1,128)S(1)} %get-tuple-element.47.refs_0_, f32[1,4096]{1,0:T(1,128)S(1)} %collective-permute-done.3.refs_1_, f32[1,4096]{1,0:T(1,128)S(1)} %collective-permute-done.4.refs_2_, f32[1,4096]{1,0:T(1,128)S(1)} %collective-permute-done.5.refs_3_, ...), custom_call_target="tpu_custom_call" | custom-call | tf_op jit(solution)/shard_map/update/pallas_call | solution.py:464
  (7 shorter events, 0.1 us)
Async XLA Ops:
  0.6 9.1 %collective-permute-start = (bf16[1,64,128]{2,1,0:T(8,128)(2,1)}, bf16[1,64,128]{2,1,0:T(8,128)(2,1)S(1)}, u32[]{:S(2)}, u32[]{:S(2)}) collective-permute-start(bf16[1,64,128]{2,1,0:T(8,128)(2,1)} %refs_5_.1), channel_id=1, source_target_pairs={{0,16},{1,17},{2,18},{3,19},{4,20},{5,21},{6,22},{7,23},{8,24},{9,... | collective-permute-start | bytes 49160 | tf_op jit(solution)/shard_map/ppermute | solution.py:318
  9.8 5.4 %collective-permute-start.1 = (bf16[10,64,128]{2,1,0:T(8,128)(2,1)S(1)}, bf16[10,64,128]{2,1,0:T(8,128)(2,1)S(1)}, u32[]{:S(2)}, u32[]{:S(2)}) collective-permute-start(bf16[10,64,128]{2,1,0:T(8,128)(2,1)S(1)} %pad_maximum_fusion), channel_id=1, source_target_pairs={{0,4},{1,9},{2,6},{3,11},{4,0},{5,13},{6,2},{7,15},{8,12},{9,1},{1... | collective-permute-start | bytes 491528 | tf_op jit(solution)/shard_map/ppermute | solution.py:318
  15.2 4.3 %collective-permute-start.6 = (f32[2,64,128]{2,1,0:T(8,128)S(1)}, f32[2,64,128]{2,1,0:T(8,128)S(1)}, u32[]{:S(2)}, u32[]{:S(2)}) collective-permute-start(f32[2,64,128]{2,1,0:T(8,128)S(1)} %slice_add_fusion), channel_id=1, source_target_pairs={{0,8},{1,5},{2,10},{3,7},{4,12},{5,1},{6,14},{7,3},{8,0},{9,13},{1... | collective-permute-start | bytes 196616 | tf_op jit(solution)/shard_map/ppermute | solution.py:318
  16.2 4.3 %collective-permute-start.2 = (bf16[4,64,128]{2,1,0:T(8,128)(2,1)S(1)}, bf16[4,64,128]{2,1,0:T(8,128)(2,1)S(1)}, u32[]{:S(2)}, u32[]{:S(2)}) collective-permute-start(bf16[4,64,128]{2,1,0:T(8,128)(2,1)S(1)} %pad_maximum_fusion.1), channel_id=1, source_target_pairs={{0,8},{1,5},{2,10},{3,7},{4,12},{5,1},{6,14},{7,3},{8,0},{9,13},{1... | collective-permute-start | bytes 196616 | tf_op jit(solution)/shard_map/ppermute | solution.py:318
  20.6 7.9 %copy-start = (bf16[1,64,4096]{2,1,0:T(8,128)(2,1)S(1)}, bf16[1,64,4096]{2,1,0:T(8,128)(2,1)}, u32[]{:S(2)}) copy-start(bf16[1,64,4096]{2,1,0:T(8,128)(2,1)} %param.7) | copy-start | bytes 1572868
  20.6 7.9 %copy-start.1 = (f32[1,4096]{1,0:T(1,128)S(1)}, f32[1,4096]{1,0:T(1,128)}, u32[]{:S(2)}) copy-start(f32[1,4096]{1,0:T(1,128)} %refs_4_.1) | copy-start | bytes 49156
  22.1 3.8 %collective-permute-start.3 = (f32[1,4096]{1,0:T(1,128)S(1)}, f32[1,4096]{1,0:T(1,128)S(1)}, u32[]{:S(2)}, u32[]{:S(2)}) collective-permute-start(f32[1,4096]{1,0:T(1,128)S(1)} %get-tuple-element.47.refs_0_), channel_id=1, source_target_pairs={{0,2},{1,3},{2,0},{3,1},{4,6},{5,7},{6,4},{7,5},{8,10},{9,11},{10,... | collective-permute-start | bytes 49160 | tf_op jit(solution)/shard_map/ppermute | solution.py:323
  23.7 4.8 %collective-permute-start.7 = (f32[1,64,128]{2,1,0:T(8,128)S(1)}, f32[1,64,128]{2,1,0:T(8,128)S(1)}, u32[]{:S(2)}, u32[]{:S(2)}) collective-permute-start(f32[1,64,128]{2,1,0:T(8,128)S(1)} %get-tuple-element.53), channel_id=1, source_target_pairs={{0,16},{1,17},{2,18},{3,19},{4,20},{5,21},{6,22},{7,23},{8,24},{9,... | collective-permute-start | bytes 98312 | tf_op jit(solution)/shard_map/ppermute | solution.py:318
  24.8 1.2 %collective-permute-start.4 = (f32[1,4096]{1,0:T(1,128)S(1)}, f32[1,4096]{1,0:T(1,128)S(1)}, u32[]{:S(2)}, u32[]{:S(2)}) collective-permute-start(f32[1,4096]{1,0:T(1,128)S(1)} %get-tuple-element.47.refs_0_), channel_id=1, source_target_pairs={{0,1},{1,0},{2,3},{3,2},{4,5},{5,4},{6,7},{7,6},{8,9},{9,8},{10,11... | collective-permute-start | bytes 49160 | tf_op jit(solution)/shard_map/ppermute | solution.py:323
  25.9 2.6 %collective-permute-start.5 = (f32[1,4096]{1,0:T(1,128)S(1)}, f32[1,4096]{1,0:T(1,128)S(1)}, u32[]{:S(2)}, u32[]{:S(2)}) collective-permute-start(f32[1,4096]{1,0:T(1,128)S(1)} %collective-permute-done.3.refs_1_), channel_id=1, source_target_pairs={{0,1},{1,0},{2,3},{3,2},{4,5},{5,4},{6,7},{7,6},{8,9},{9,8},{10,11... | collective-permute-start | bytes 49160 | tf_op jit(solution)/shard_map/ppermute | solution.py:323
